TPU v7x, 32 devices: a whole 2x2x4 slice. The times are simulated.
32 devices in a mesh: section: 2 (over core), dp: 4 (over z), tensor: 4 (over y, x).
Axes of the slice: x: 2, y: 2, z: 4, core: 2. Of those that a mesh axis runs over, the one named last changes fastest.
Arguments:
- inputs: bfloat16 [1024, 8, 1024], P('tensor', 'dp'), may hold values from -6 to 6
- segments: int32 [8, 1024], P('dp'), may hold values from 0 to 3, never falling along the last dimension, each value on 1 to 512 neighbouring positions
- cotangent: bfloat16 [1024, 8, 1024], P('tensor', 'dp'), may hold values from -6 to 6
- gain_attn: float32 [2, 1024], P('section'), may hold values from 0.1 to 1.9
- joint_projection_weight: bfloat16 [2, 1024, 3, 1024], P('section', None, None, 'tensor'), may hold values from -0.1875 to 0.1875
- query_down_factor: bfloat16 [2, 1024, 4], P('section'), may hold values from -0.1875 to 0.1875
- query_up_factor: bfloat16 [2, 4, 1024], P('section', None, 'tensor'), may hold values from -0.1875 to 0.1875
- value_down_factor: bfloat16 [2, 1024, 4], P('section'), may hold values from -0.1875 to 0.1875
- value_up_factor: bfloat16 [2, 4, 1024], P('section', None, 'tensor'), may hold values from -0.1875 to 0.1875
- w_out: bfloat16 [2, 1024, 1024], P('section', 'tensor'), may hold values from -1.5 to 1.5
- gain_mlp: float32 [2, 1024], P('section'), may hold values from 0.1 to 1.9
- w_fc: bfloat16 [2, 1024, 4096], P('section', None, 'tensor'), may hold values from -0.1875 to 0.1875
- w_proj: bfloat16 [2, 4096, 1024], P('section', 'tensor'), may hold values from -0.09375 to 0.09375
Outputs:
- activations: bfloat16 [2, 1024, 8, 1024], P('section', 'tensor', 'dp')
- input_grads: bfloat16 [2, 1024, 8, 1024], P('section', 'tensor', 'dp')
- grad_a_query: float32 [2, 1024, 4], P('section')
- grad_b_query: float32 [2, 4, 1024], P('section')
- grad_a_value: float32 [2, 1024, 4], P('section')
- grad_b_value: float32 [2, 4, 1024], P('section')
Inputs may be any that keep to these rules, and one draw needn't show every extreme that they name: `segments`: along a row the segment numbers never fall; a segment holds at most 512 slots of a row, and some segment holds exactly that many.
All inputs are finite; a program needn't handle non-finite values.
Results may differ from a plain program's by a relative error of at most 0.034.
Values may be sent and summed in bfloat16 or wider, within the bound.
A program may use at most 128 MiB of HBM per device.

v0:
```python
import jax
import jax.numpy as jnp
from jax import lax
from jax.sharding import PartitionSpec as P

HEAD_DIM = 64
MICRO = 2


EPSILON = 1e-05
PRECISE = lax.Precision.HIGHEST
MASKED = -1000000000.0
CUBIC_TERM = 0.044715
TANH_SCALE = 0.7978845608028654


def passed_along(block, axis, distance):
    devices = range(lax.axis_size(axis))
    route = [(i - distance, i) for i in devices if i - distance in devices]
    return lax.ppermute(block, axis, route)


def gelu_tanh(value):
    return 0.5 * value * (1.0 + jnp.tanh(TANH_SCALE * (value + CUBIC_TERM * value * value * value)))


def normalize(residual_stream, gain):
    middle = jnp.mean(residual_stream, axis=-1, keepdims=True)
    centred = residual_stream - middle
    inverse = lax.rsqrt(jnp.mean(centred * centred, axis=-1, keepdims=True) + EPSILON)
    unit_rows = centred * inverse
    return (unit_rows * gain, unit_rows, inverse)


def normalize_back(grad_norm, unit_rows, inverse, gain):
    scaled = grad_norm * gain
    return inverse * (
        scaled
        - jnp.mean(scaled, axis=-1, keepdims=True)
        - unit_rows * jnp.mean(scaled * unit_rows, axis=-1, keepdims=True)
    )


def block_mask(segment_row_span, first_row, block):
    length = segment_row_span.shape[1]
    segment_part = lax.dynamic_slice_in_dim(segment_row_span, first_row, block, 1)
    query_places = first_row + jnp.arange(block)
    key_places = jnp.arange(length)
    same_doc = segment_part[:, :, None] == segment_row_span[:, None, :]
    return same_doc & (key_places[None, None, :] <= query_places[None, :, None])


def projected_rows(row_portion, joint_projection_weight, adapter_pair):
    query_down_factor, query_up_factor, value_down_factor, value_up_factor = adapter_pair
    factor = 32.0 / query_down_factor.shape[-1]
    joined = jnp.einsum(
        "srd,dcf->srcf", row_portion, joint_projection_weight, preferred_element_type=jnp.float32
    )
    narrow_query_rows = jnp.einsum(
        "srd,dk->srk", row_portion, query_down_factor, preferred_element_type=jnp.float32
    )
    narrow_value_rows = jnp.einsum(
        "srd,dk->srk", row_portion, value_down_factor, preferred_element_type=jnp.float32
    )
    queries = joined[:, :, 0] + factor * jnp.einsum(
        "srk,kf->srf", narrow_query_rows, query_up_factor.astype(jnp.float32), precision=PRECISE
    )
    values_all = joined[:, :, 2] + factor * jnp.einsum(
        "srk,kf->srf", narrow_value_rows, value_up_factor.astype(jnp.float32), precision=PRECISE
    )
    stacked_weights = jnp.stack([queries, joined[:, :, 1], values_all], axis=2).astype(jnp.bfloat16)
    return (stacked_weights, narrow_query_rows, narrow_value_rows)


def attention_forward(queries, keys_all, values_all, segment_row_span):
    length, row_count, head_count, width = queries.shape
    block = min(512, length)
    factor = width ** (-0.5)

    def one_block(block_index):
        first_row = block_index * block
        query_part = lax.dynamic_slice_in_dim(queries, first_row, block, 0)
        scores = (
            jnp.einsum("qrhe,krhe->rhqk", query_part, keys_all, preferred_element_type=jnp.float32)
            * factor
        )
        allowed = block_mask(segment_row_span, first_row, block)
        scores = jnp.where(allowed[:, None], scores, MASKED)
        row_max = jnp.max(scores, axis=-1, keepdims=True)
        exponent = jnp.exp(scores - row_max)
        total = jnp.sum(exponent, axis=-1, keepdims=True)
        weights_soft = (exponent / total).astype(jnp.bfloat16)
        attended = jnp.einsum(
            "rhqk,krhe->qrhe", weights_soft, values_all, preferred_element_type=jnp.float32
        )
        return (attended, (row_max + jnp.log(total))[..., 0])

    attended, log_sums = lax.map(one_block, jnp.arange(length // block))
    attended = attended.reshape(length, row_count, head_count, width)
    log_sums = jnp.moveaxis(log_sums, 0, 2).reshape(row_count, head_count, length)
    return (attended, log_sums)


def attention_backward(queries, keys_all, values_all, segment_row_span, log_sums, grad_heads):
    length = queries.shape[0]
    block = min(512, length)
    factor = queries.shape[-1] ** (-0.5)

    def one_block(carry, block_index):
        grad_keys, grad_values = carry
        first_row = block_index * block
        query_part = lax.dynamic_slice_in_dim(queries, first_row, block, 0)
        grad_part = lax.dynamic_slice_in_dim(grad_heads, first_row, block, 0)
        sums_part = lax.dynamic_slice_in_dim(log_sums, first_row, block, 2)
        scores = (
            jnp.einsum("qrhe,krhe->rhqk", query_part, keys_all, preferred_element_type=jnp.float32)
            * factor
        )
        allowed = block_mask(segment_row_span, first_row, block)
        scores = jnp.where(allowed[:, None], scores, MASKED)
        weights_soft = jnp.exp(scores - sums_part[..., None])
        grad_soft = jnp.einsum(
            "qrhe,krhe->rhqk", grad_part, values_all, preferred_element_type=jnp.float32
        )
        grad_scores = weights_soft * (
            grad_soft - jnp.sum(weights_soft * grad_soft, axis=-1, keepdims=True)
        )
        grad_scores = grad_scores.astype(jnp.bfloat16)
        grad_query = (
            jnp.einsum("rhqk,krhe->qrhe", grad_scores, keys_all, preferred_element_type=jnp.float32)
            * factor
        )
        grad_keys = (
            grad_keys
            + jnp.einsum(
                "rhqk,qrhe->krhe", grad_scores, query_part, preferred_element_type=jnp.float32
            )
            * factor
        )
        grad_values = grad_values + jnp.einsum(
            "rhqk,qrhe->krhe",
            weights_soft.astype(jnp.bfloat16),
            grad_part,
            preferred_element_type=jnp.float32,
        )
        return ((grad_keys, grad_values), grad_query)

    start_state = (jnp.zeros(keys_all.shape, jnp.float32), jnp.zeros(values_all.shape, jnp.float32))
    (grad_keys, grad_values), grad_blocks = lax.scan(
        one_block, start_state, jnp.arange(length // block)
    )
    return (grad_blocks.reshape(queries.shape), grad_keys, grad_values)


def attend_all(stacked_weights, segment_row_span):
    length, row_count = (stacked_weights.shape[0], stacked_weights.shape[1])
    head_view = stacked_weights.reshape(length, row_count, 3, -1, HEAD_DIM)
    queries, keys_all, values_all = (head_view[:, :, 0], head_view[:, :, 1], head_view[:, :, 2])
    attended, log_sums = attention_forward(queries, keys_all, values_all, segment_row_span)
    return (
        attended.reshape(length, row_count, -1).astype(jnp.bfloat16),
        log_sums,
        (queries, keys_all, values_all),
    )


def attention_project(attended_b, w_out):
    return lax.psum_scatter(
        jnp.einsum("srf,fd->srd", attended_b, w_out, preferred_element_type=jnp.float32).astype(
            jnp.bfloat16
        ),
        "tensor",
        scatter_dimension=0,
        tiled=True,
    ).astype(jnp.float32)


def attention_grad_heads(grad_middle_b, w_out):
    grad_attended = jnp.einsum(
        "srd,fd->srf",
        lax.all_gather(grad_middle_b, "tensor", axis=0, tiled=True),
        w_out,
        preferred_element_type=jnp.float32,
    )
    return grad_attended.astype(jnp.bfloat16)


def mlp_pre(normed_b, w_fc):
    return jnp.einsum(
        "srd,df->srf",
        lax.all_gather(normed_b, "tensor", axis=0, tiled=True),
        w_fc,
        preferred_element_type=jnp.float32,
    )


def mlp_out(hidden_b, w_proj):
    return lax.psum_scatter(
        jnp.einsum("srf,fd->srd", hidden_b, w_proj, preferred_element_type=jnp.float32).astype(
            jnp.bfloat16
        ),
        "tensor",
        scatter_dimension=0,
        tiled=True,
    ).astype(jnp.float32)


def mlp_back(grad_mlp, pre_act, w_fc, w_proj):
    grad_hidden = jnp.einsum(
        "srd,fd->srf",
        lax.all_gather(grad_mlp, "tensor", axis=0, tiled=True),
        w_proj,
        preferred_element_type=jnp.float32,
    )
    activated, slope = jax.vjp(gelu_tanh, pre_act)
    grad_pre = slope(grad_hidden)[0].astype(jnp.bfloat16)
    return lax.psum_scatter(
        jnp.einsum("srf,df->srd", grad_pre, w_fc, preferred_element_type=jnp.float32).astype(
            jnp.bfloat16
        ),
        "tensor",
        scatter_dimension=0,
        tiled=True,
    ).astype(jnp.float32)


def forward_layer_step(layer_input_rows, segment_row_span, fixed_weights, adapter_pair):
    norm_rows = normalize(layer_input_rows, fixed_weights[0])[0].astype(jnp.bfloat16)
    stacked_weights = projected_rows(
        lax.all_gather(norm_rows, "tensor", axis=0, tiled=True), fixed_weights[1], adapter_pair
    )[0]
    attended_b = attend_all(stacked_weights, segment_row_span)[0]
    middle = layer_input_rows + attention_project(attended_b, fixed_weights[2])
    normed_mlp = normalize(middle, fixed_weights[3])[0].astype(jnp.bfloat16)
    pre_act = mlp_pre(normed_mlp, fixed_weights[4])
    hidden_b = gelu_tanh(pre_act).astype(jnp.bfloat16)
    return middle + mlp_out(hidden_b, fixed_weights[5])


def backward_layer_step(
    layer_input_rows, segment_row_span, upstream_gradient, fixed_weights, adapter_pair
):
    gain_a, joint_projection_weight, w_out, gain_m, w_fc, w_proj = fixed_weights
    query_down_factor, query_up_factor, value_down_factor, value_up_factor = adapter_pair
    factor = 32.0 / query_down_factor.shape[-1]
    norm_rows, unit_first, inverse_first = normalize(layer_input_rows, gain_a)
    collected_rows = lax.all_gather(norm_rows.astype(jnp.bfloat16), "tensor", axis=0, tiled=True)
    stacked_weights, narrow_query_rows, narrow_value_rows = projected_rows(
        collected_rows, joint_projection_weight, adapter_pair
    )
    length, row_count = (collected_rows.shape[0], collected_rows.shape[1])
    attended_b, log_sums, head_views = attend_all(stacked_weights, segment_row_span)
    queries, keys_all, values_all = head_views
    middle = layer_input_rows + attention_project(attended_b, w_out)
    normed_mlp, unit_second, inverse_second = normalize(middle, gain_m)
    pre_act = mlp_pre(normed_mlp.astype(jnp.bfloat16), w_fc)
    grad_norm_mlp = mlp_back(upstream_gradient.astype(jnp.bfloat16), pre_act, w_fc, w_proj)
    grad_middle = upstream_gradient + normalize_back(
        grad_norm_mlp, unit_second, inverse_second, gain_m
    )
    grad_attended = attention_grad_heads(grad_middle.astype(jnp.bfloat16), w_out)
    grad_heads = grad_attended.reshape(queries.shape)
    grad_queries, grad_keys, grad_values = attention_backward(
        queries, keys_all, values_all, segment_row_span, log_sums, grad_heads
    )
    grad_stack = (
        jnp.stack([grad_queries, grad_keys, grad_values], axis=2)
        .astype(jnp.bfloat16)
        .reshape(length, row_count, 3, -1)
    )
    grad_query_rows = grad_stack[:, :, 0]
    grad_value_rows = grad_stack[:, :, 2]
    thin_grad_query = factor * jnp.einsum(
        "srf,kf->srk", grad_query_rows, query_up_factor, preferred_element_type=jnp.float32
    )
    thin_grad_value = factor * jnp.einsum(
        "srf,kf->srk", grad_value_rows, value_up_factor, preferred_element_type=jnp.float32
    )
    grad_bq = factor * jnp.einsum(
        "srk,srf->kf", narrow_query_rows, grad_query_rows.astype(jnp.float32), precision=PRECISE
    )
    grad_bv = factor * jnp.einsum(
        "srk,srf->kf", narrow_value_rows, grad_value_rows.astype(jnp.float32), precision=PRECISE
    )
    gathered_wide = collected_rows.astype(jnp.float32)
    grad_aq = jnp.einsum("srd,srk->dk", gathered_wide, thin_grad_query, precision=PRECISE)
    grad_av = jnp.einsum("srd,srk->dk", gathered_wide, thin_grad_value, precision=PRECISE)
    a_query_wide = query_down_factor.astype(jnp.float32)
    a_value_wide = value_down_factor.astype(jnp.float32)
    term = jnp.einsum(
        "srcf,dcf->srd", grad_stack, joint_projection_weight, preferred_element_type=jnp.float32
    )
    term = term + jnp.einsum("srk,dk->srd", thin_grad_query, a_query_wide, precision=PRECISE)
    grad_norm_attn = lax.psum_scatter(
        (term + jnp.einsum("srk,dk->srd", thin_grad_value, a_value_wide, precision=PRECISE)).astype(
            jnp.bfloat16
        ),
        "tensor",
        scatter_dimension=0,
        tiled=True,
    ).astype(jnp.float32)
    layer_output_rows = grad_middle + normalize_back(
        grad_norm_attn, unit_first, inverse_first, gain_a
    )
    return (layer_output_rows, (grad_aq, grad_bq, grad_av, grad_bv))


def body(
    inputs,
    segments,
    cotangent,
    gain_attn,
    joint_projection_weight,
    query_down_factor,
    query_up_factor,
    value_down_factor,
    value_up_factor,
    w_out,
    gain_mlp,
    w_fc,
    w_proj,
):
    fixed_weights = (
        gain_attn[0],
        joint_projection_weight[0],
        w_out[0],
        gain_mlp[0],
        w_fc[0],
        w_proj[0],
    )
    adapter_pair = (
        query_down_factor[0],
        query_up_factor[0],
        value_down_factor[0],
        value_up_factor[0],
    )
    sections = lax.axis_size("section")
    section_index = lax.axis_index("section")
    is_first = section_index == 0
    is_last = section_index == sections - 1
    rows_mb = inputs.shape[1] // MICRO
    ticks = MICRO + sections - 1
    block_shape = (inputs.shape[0], rows_mb, inputs.shape[2])
    activations = jnp.zeros_like(inputs)
    kept_inputs = jnp.zeros((MICRO,) + block_shape, jnp.bfloat16)
    arriving = jnp.zeros(block_shape, jnp.bfloat16)
    for tick_index in range(ticks):
        own_index = min(tick_index, MICRO - 1)
        mb_slot = tick_index - section_index
        is_valid = (mb_slot >= 0) & (mb_slot < MICRO)
        mb_slot = jnp.clip(mb_slot, 0, MICRO - 1)
        fresh = lax.slice_in_dim(inputs, own_index * rows_mb, (own_index + 1) * rows_mb, axis=1)
        layer_input_rows = jnp.where(is_first, fresh, arriving)
        segment_row_span = lax.dynamic_slice_in_dim(segments, mb_slot * rows_mb, rows_mb, 0)
        layer_output_rows = forward_layer_step(
            layer_input_rows.astype(jnp.float32), segment_row_span, fixed_weights, adapter_pair
        ).astype(jnp.bfloat16)
        activations = jnp.where(
            is_valid,
            lax.dynamic_update_slice_in_dim(activations, layer_output_rows, mb_slot * rows_mb, 1),
            activations,
        )
        kept_inputs = jnp.where(
            is_valid, kept_inputs.at[mb_slot].set(layer_input_rows), kept_inputs
        )
        if tick_index < ticks - 1:
            arriving = passed_along(layer_output_rows, "section", 1)
    input_grads = jnp.zeros_like(inputs)
    gradient_totals = tuple(
        (jnp.zeros(factor_tensor.shape, jnp.float32) for factor_tensor in adapter_pair)
    )
    arriving = jnp.zeros(block_shape, jnp.bfloat16)
    for tick_index in range(ticks):
        own_index = min(tick_index, MICRO - 1)
        mb_slot = tick_index - (sections - 1 - section_index)
        is_valid = (mb_slot >= 0) & (mb_slot < MICRO)
        mb_slot = jnp.clip(mb_slot, 0, MICRO - 1)
        given = lax.slice_in_dim(cotangent, own_index * rows_mb, (own_index + 1) * rows_mb, axis=1)
        upstream_gradient = jnp.where(is_last, given, arriving).astype(jnp.float32)
        layer_input_rows = kept_inputs[mb_slot].astype(jnp.float32)
        segment_row_span = lax.dynamic_slice_in_dim(segments, mb_slot * rows_mb, rows_mb, 0)
        layer_output_rows, row_pieces = backward_layer_step(
            layer_input_rows, segment_row_span, upstream_gradient, fixed_weights, adapter_pair
        )
        leaving_b = layer_output_rows.astype(jnp.bfloat16)
        input_grads = jnp.where(
            is_valid,
            lax.dynamic_update_slice_in_dim(input_grads, leaving_b, mb_slot * rows_mb, 1),
            input_grads,
        )
        gradient_totals = tuple(
            (
                running + jnp.where(is_valid, piece_grad, 0.0)
                for running, piece_grad in zip(gradient_totals, row_pieces)
            )
        )
        if tick_index < ticks - 1:
            arriving = passed_along(leaving_b, "section", -1)
    adapter_rank = adapter_pair[1].shape[0]
    model_width = inputs.shape[2]
    column_total = adapter_pair[1].shape[1]
    offset = lax.axis_index("tensor") * column_total
    full_query = lax.dynamic_update_slice_in_dim(
        jnp.zeros((adapter_rank, model_width), jnp.float32), gradient_totals[1], offset, 1
    )
    full_value = lax.dynamic_update_slice_in_dim(
        jnp.zeros((adapter_rank, model_width), jnp.float32), gradient_totals[3], offset, 1
    )
    summed = lax.psum(
        (gradient_totals[0], full_query, gradient_totals[2], full_value), ("dp", "tensor")
    )
    return (
        activations[None],
        input_grads[None],
        summed[0][None],
        summed[1][None],
        summed[2][None],
        summed[3][None],
    )


def solution(mesh):
    placed = (
        P("tensor", "dp", None),
        P("dp", None),
        P("tensor", "dp", None),
        P("section", None),
        P("section", None, None, "tensor"),
        P("section", None, None),
        P("section", None, "tensor"),
        P("section", None, None),
        P("section", None, "tensor"),
        P("section", "tensor", None),
        P("section", None),
        P("section", None, "tensor"),
        P("section", "tensor", None),
    )
    return jax.shard_map(
        body,
        mesh=mesh,
        in_specs=placed,
        out_specs=(
            P("section", "tensor", "dp", None),
            P("section", "tensor", "dp", None),
            P("section", None, None),
            P("section", None, None),
            P("section", None, None),
            P("section", None, None),
        ),
        check_vma=False,
    )
```

profile of v0, /device:TPU:0, one launch (start us, length us, event | category | flops | bytes accessed | tf_op | source)
XLA Modules:
  0.0 1891.0 jit_solution(14451011114471732137)
XLA Ops:
  17.2 37.5 %all-gather.19.cloned.1.call-done = bf16[1024,1,1024]{2,0,1:T(8,128)(2,1)} async-done(((bf16[256,1,1024]{2,0,1:T(8,128)(2,1)}), bf16[1024,1,1024]{2,0,1:T(8,128)(2,1)}) %all-gather.19.cloned.1.call-update) | async-done | bytes 2097168 | tf_op jit(solution)/shard_map/all_gather | solution.py:230
  101.4 35.3 %reduce-scatter.16.cloned.1.call-done = bf16[256,1,1024]{2,0,1:T(8,128)(2,1)} async-done(((bf16[1024,1,1024]{2,0,1:T(8,128)(2,1)}), bf16[256,1,1024]{2,0,1:T(8,128)(2,1)}) %reduce-scatter.16.cloned.1.call-update) | async-done | bytes 524304 | tf_op jit(solution)/shard_map/reduce_scatter | solution.py:168
  142.2 35.2 %all-gather.21.cloned.1.call-done = bf16[1024,1,1024]{2,0,1:T(8,128)(2,1)} async-done(((bf16[256,1,1024]{2,0,1:T(8,128)(2,1)}), bf16[1024,1,1024]{2,0,1:T(8,128)(2,1)}) %all-gather.21.cloned.1.call-update) | async-done | bytes 2097168 | tf_op jit(solution)/shard_map/all_gather | solution.py:191
  185.6 35.3 %reduce-scatter.18.cloned.1.call-done = bf16[256,1,1024]{2,0,1:T(8,128)(2,1)} async-done(((bf16[1024,1,1024]{2,0,1:T(8,128)(2,1)}), bf16[256,1,1024]{2,0,1:T(8,128)(2,1)}) %reduce-scatter.18.cloned.1.call-update) | async-done | bytes 524304 | tf_op jit(solution)/shard_map/reduce_scatter | solution.py:198
  232.6 35.6 %all-gather.23.cloned.1.call-done = bf16[1024,1,1024]{2,0,1:T(8,128)(2,1)} async-done(((bf16[256,1,1024]{2,0,1:T(8,128)(2,1)}), bf16[1024,1,1024]{2,0,1:T(8,128)(2,1)}) %all-gather.23.cloned.1.call-update) | async-done | bytes 2097168 | tf_op jit(solution)/shard_map/all_gather | solution.py:230
  314.9 35.3 %reduce-scatter.20.cloned.1.call-done = bf16[256,1,1024]{2,0,1:T(8,128)(2,1)} async-done(((bf16[1024,1,1024]{2,0,1:T(8,128)(2,1)}), bf16[256,1,1024]{2,0,1:T(8,128)(2,1)}) %reduce-scatter.20.cloned.1.call-update) | async-done | bytes 524304 | tf_op jit(solution)/shard_map/reduce_scatter | solution.py:168
  399.1 35.3 %reduce-scatter.22.cloned.1.call-done = bf16[256,1,1024]{2,0,1:T(8,128)(2,1)} async-done(((bf16[1024,1,1024]{2,0,1:T(8,128)(2,1)}), bf16[256,1,1024]{2,0,1:T(8,128)(2,1)}) %reduce-scatter.22.cloned.1.call-update) | async-done | bytes 524304 | tf_op jit(solution)/shard_map/reduce_scatter | solution.py:198
  445.8 35.6 %all-gather.47.cloned.1.call-done = bf16[1024,1,1024]{2,0,1:T(8,128)(2,1)} async-done(((bf16[256,1,1024]{2,0,1:T(8,128)(2,1)}), bf16[1024,1,1024]{2,0,1:T(8,128)(2,1)}) %all-gather.47.cloned.1.call-update) | async-done | bytes 2097168 | tf_op jit(solution)/shard_map/all_gather | solution.py:247
  518.4 35.3 %reduce-scatter.40.cloned.1.call-done = bf16[256,1,1024]{2,0,1:T(8,128)(2,1)} async-done(((bf16[1024,1,1024]{2,0,1:T(8,128)(2,1)}), bf16[256,1,1024]{2,0,1:T(8,128)(2,1)}) %reduce-scatter.40.cloned.1.call-update) | async-done | bytes 524304 | tf_op jit(solution)/shard_map/reduce_scatter | solution.py:168
  668.5 38.0 %reduce-scatter.28.cloned.1.call-done = bf16[256,1,1024]{2,0,1:T(8,128)(2,1)} async-done(((bf16[1024,1,1024]{2,0,1:T(8,128)(2,1)}), bf16[256,1,1024]{2,0,1:T(8,128)(2,1)}) %reduce-scatter.28.cloned.1.call-update) | async-done | bytes 524304 | tf_op jit(solution)/shard_map/reduce_scatter | solution.py:168
  793.8 35.3 %reduce-scatter.30.cloned.1.call-done = bf16[256,1,1024]{2,0,1:T(8,128)(2,1)} async-done(((bf16[1024,1,1024]{2,0,1:T(8,128)(2,1)}), bf16[256,1,1024]{2,0,1:T(8,128)(2,1)}) %reduce-scatter.30.cloned.1.call-update) | async-done | bytes 524304 | tf_op jit(solution)/shard_map/reduce_scatter | solution.py:217
  835.4 35.2 %all-gather.37.cloned.1.call-done = bf16[1024,1,1024]{2,0,1:T(8,128)(2,1)} async-done(((bf16[256,1,1024]{2,0,1:T(8,128)(2,1)}), bf16[1024,1,1024]{2,0,1:T(8,128)(2,1)}) %all-gather.37.cloned.1.call-update) | async-done | bytes 2097168 | tf_op jit(solution)/shard_map/all_gather | solution.py:181
  874.6 52.0 %while.120 = (s32[]{:T(128)}, f32[1024,1,4,64]{0,3,2,1:T(8,128)}, f32[1024,1,4,64]{0,3,2,1:T(8,128)}, bf16[2,512,1,4,64]{1,4,3,2,0:T(8,128)(2,1)}, s32[2]{0:T(12...) while((s32[]{:T(128)}, f32[1024,1,4,64]{0,3,2,1:T(8,128)}, ...), condition=%wide.region_47.48_spmd.clone, body=%wide.region_45.47_spmd.clone.sunk | while | flops 1376647680 | bytes 147921840 | solution.py:149
  960.5 35.3 %reduce-scatter.32.cloned.1.call-done = bf16[256,1,1024]{2,0,1:T(8,128)(2,1)} async-done(((bf16[1024,1,1024]{2,0,1:T(8,128)(2,1)}), bf16[256,1,1024]{2,0,1:T(8,128)(2,1)}) %reduce-scatter.32.cloned.1.call-update) | async-done | bytes 524304 | tf_op jit(solution)/shard_map/reduce_scatter | solution.py:294
  1082.9 35.3 %reduce-scatter.36.cloned.1.call-done = bf16[256,1,1024]{2,0,1:T(8,128)(2,1)} async-done(((bf16[1024,1,1024]{2,0,1:T(8,128)(2,1)}), bf16[256,1,1024]{2,0,1:T(8,128)(2,1)}) %reduce-scatter.36.cloned.1.call-update) | async-done | bytes 524304 | tf_op jit(solution)/shard_map/reduce_scatter | solution.py:217
  1123.0 35.4 %all-gather.45.cloned.1.call-done = bf16[1024,1,1024]{2,0,1:T(8,128)(2,1)} async-done(((bf16[256,1,1024]{2,0,1:T(8,128)(2,1)}), bf16[1024,1,1024]{2,0,1:T(8,128)(2,1)}) %all-gather.45.cloned.1.call-update) | async-done | bytes 2097168 | tf_op jit(solution)/shard_map/all_gather | solution.py:181
  1162.6 49.2 %while.121 = (s32[]{:T(128)}, f32[1024,1,4,64]{0,3,2,1:T(8,128)}, f32[1024,1,4,64]{0,3,2,1:T(8,128)}, bf16[2,512,1,4,64]{1,4,3,2,0:T(8,128)(2,1)}, s32[2]{0:T(12...) while((s32[]{:T(128)}, f32[1024,1,4,64]{0,3,2,1:T(8,128)}, ...), condition=%wide.region_65.66_spmd.clone, body=%wide.region_63.65_spmd.clone.sunk | while | flops 1376647680 | bytes 156310064 | solution.py:149
  1366.3 35.3 %reduce-scatter.42.cloned.1.call-done = bf16[256,1,1024]{2,0,1:T(8,128)(2,1)} async-done(((bf16[1024,1,1024]{2,0,1:T(8,128)(2,1)}), bf16[256,1,1024]{2,0,1:T(8,128)(2,1)}) %reduce-scatter.42.cloned.1.call-update) | async-done | bytes 524304 | tf_op jit(solution)/shard_map/reduce_scatter | solution.py:217
  1406.5 35.4 %all-gather.53.cloned.1.call-done = bf16[1024,1,1024]{2,0,1:T(8,128)(2,1)} async-done(((bf16[256,1,1024]{2,0,1:T(8,128)(2,1)}), bf16[1024,1,1024]{2,0,1:T(8,128)(2,1)}) %all-gather.53.cloned.1.call-update) | async-done | bytes 2097168 | tf_op jit(solution)/shard_map/all_gather | solution.py:181
  1445.9 49.2 %while.122 = (s32[]{:T(128)}, f32[1024,1,4,64]{0,3,2,1:T(8,128)}, f32[1024,1,4,64]{0,3,2,1:T(8,128)}, bf16[2,512,1,4,64]{1,4,3,2,0:T(8,128)(2,1)}, s32[2]{0:T(12...) while((s32[]{:T(128)}, f32[1024,1,4,64]{0,3,2,1:T(8,128)}, ...), condition=%wide.region_83.84_spmd.clone, body=%wide.region_81.83_spmd.clone.sunk | while | flops 1376647680 | bytes 156310064 | solution.py:149
  1566.9 35.0 %all-gather.27.cloned.1.call-done = bf16[1024,1,1024]{2,0,1:T(8,128)(2,1)} async-done(((bf16[256,1,1024]{2,0,1:T(8,128)(2,1)}), bf16[1024,1,1024]{2,0,1:T(8,128)(2,1)}) %all-gather.27.cloned.1.call-update) | async-done | bytes 2097168 | tf_op jit(solution)/shard_map/all_gather | solution.py:230
  1648.3 35.3 %reduce-scatter.24.cloned.1.call-done = bf16[256,1,1024]{2,0,1:T(8,128)(2,1)} async-done(((bf16[1024,1,1024]{2,0,1:T(8,128)(2,1)}), bf16[256,1,1024]{2,0,1:T(8,128)(2,1)}) %reduce-scatter.24.cloned.1.call-update) | async-done | bytes 524304 | tf_op jit(solution)/shard_map/reduce_scatter | solution.py:168
  1689.1 35.2 %all-gather.29.cloned.1.call-done = bf16[1024,1,1024]{2,0,1:T(8,128)(2,1)} async-done(((bf16[256,1,1024]{2,0,1:T(8,128)(2,1)}), bf16[1024,1,1024]{2,0,1:T(8,128)(2,1)}) %all-gather.29.cloned.1.call-update) | async-done | bytes 2097168 | tf_op jit(solution)/shard_map/all_gather | solution.py:191
  1773.8 104.8 %all-reduce.3.cloned.1.call-done = (f32[1,1024,4]{1,2,0:T(4,128)}, f32[1,4,1024]{2,1,0:T(4,128)}, f32[1,1024,4]{1,2,0:T(4,128)}, f32[1,4,1024]{2,1,0:T(4,128)}) async-done(((f32[1,1024,4]{1,2,0:T(4,128)}, f32[1,4,1024]{2,1,0:T(4,128)}, f32[1,1024,4]{1,2,0:T(4,128)}, f32[1,4,1024]{2,1,0:T(4,128)}), (f32[1,1024,4]{1,2,0:T(4,128)}, f32[1,4,1024]{2,1,0:T(4,128)}, f32[1,1024,4]{1,2,0:T(4,128)}, ...) | async-done | bytes 65552 | tf_op jit(solution)/shard_map/psum | solution.py:409
  (783 shorter events, 1206.6 us)
Async XLA Ops:
  16.4 120.2 %reduce-scatter.16.cloned.1.call-start = ((), (), s32[]{:S(2)}) async-start(), calls=%async_computation.16 | async-start | bytes 2621440 | tf_op jit(solution)/shard_map/reduce_scatter | solution.py:168
  101.3 76.0 %all-gather.21.cloned.1.call-start = ((), (), s32[]{:S(2)}) async-start(), calls=%async_computation.17 | async-start | bytes 2621440 | tf_op jit(solution)/shard_map/all_gather | solution.py:191
  141.9 79.0 %reduce-scatter.18.cloned.1.call-start = ((), (), s32[]{:S(2)}) async-start(), calls=%async_computation.18 | async-start | bytes 2621440 | tf_op jit(solution)/shard_map/reduce_scatter | solution.py:198
  185.5 82.6 %all-gather.23.cloned.1.call-start = ((), (), s32[]{:S(2)}) async-start(), calls=%async_computation.19 | async-start | bytes 2621440 | tf_op jit(solution)/shard_map/all_gather | solution.py:230
  232.5 117.7 %reduce-scatter.20.cloned.1.call-start = ((), (), s32[]{:S(2)}) async-start(), calls=%async_computation.20 | async-start | bytes 2621440 | tf_op jit(solution)/shard_map/reduce_scatter | solution.py:168
  314.8 76.0 %all-gather.25.cloned.1.call-start = ((), (), s32[]{:S(2)}) async-start(), calls=%async_computation.21 | async-start | bytes 2621440 | tf_op jit(solution)/shard_map/all_gather | solution.py:191
  355.4 79.0 %reduce-scatter.22.cloned.1.call-start = ((), (), s32[]{:S(2)}) async-start(), calls=%async_computation.22 | async-start | bytes 2621440 | tf_op jit(solution)/shard_map/reduce_scatter | solution.py:198
  399.0 82.4 %all-gather.47.cloned.1.call-start = ((), (), s32[]{:S(2)}) async-start(), calls=%async_computation.41 | async-start | bytes 2621440 | tf_op jit(solution)/shard_map/all_gather | solution.py:247
  445.8 107.9 %reduce-scatter.40.cloned.1.call-start = ((), (), s32[]{:S(2)}) async-start(), calls=%async_computation.42 | async-start | bytes 2621440 | tf_op jit(solution)/shard_map/reduce_scatter | solution.py:168
  557.7 110.7 %reduce-scatter.34.cloned.1.call-start = ((), (), s32[]{:S(2)}) async-start(), calls=%async_computation.35 | async-start | bytes 2621440 | tf_op jit(solution)/shard_map/reduce_scatter | solution.py:168
  628.4 78.0 %reduce-scatter.28.cloned.1.call-start = ((), (), s32[]{:S(2)}) async-start(), calls=%async_computation.28 | async-start | bytes 2621440 | tf_op jit(solution)/shard_map/reduce_scatter | solution.py:168
  668.4 78.0 %all-gather.33.cloned.1.call-start = ((), (), s32[]{:S(2)}) async-start(), calls=%async_computation.29 | async-start | bytes 2621440 | tf_op jit(solution)/shard_map/all_gather | solution.py:191
  717.2 111.8 %reduce-scatter.30.cloned.1.call-start = ((), (), s32[]{:S(2)}) async-start(), calls=%async_computation.31 | async-start | bytes 2621440 | tf_op jit(solution)/shard_map/reduce_scatter | solution.py:217
  793.7 76.8 %all-gather.37.cloned.1.call-start = ((), (), s32[]{:S(2)}) async-start(), calls=%async_computation.32 | async-start | bytes 2621440 | tf_op jit(solution)/shard_map/all_gather | solution.py:181
  835.1 160.7 %reduce-scatter.32.cloned.1.call-start = ((), (), s32[]{:S(2)}) async-start(), calls=%async_computation.33 | async-start | bytes 2621440 | tf_op jit(solution)/shard_map/reduce_scatter | solution.py:294
  1008.4 109.8 %reduce-scatter.36.cloned.1.call-start = ((), (), s32[]{:S(2)}) async-start(), calls=%async_computation.38 | async-start | bytes 2621440 | tf_op jit(solution)/shard_map/reduce_scatter | solution.py:217
  1123.0 157.8 %reduce-scatter.38.cloned.1.call-start = ((), (), s32[]{:S(2)}) async-start(), calls=%async_computation.40 | async-start | bytes 2621440 | tf_op jit(solution)/shard_map/reduce_scatter | solution.py:294
  1246.2 109.7 %all-gather.51.cloned.1.call-start = ((), (), s32[]{:S(2)}) async-start(), calls=%async_computation.44 | async-start | bytes 2621440 | tf_op jit(solution)/shard_map/all_gather | solution.py:211
  1290.0 111.6 %reduce-scatter.42.cloned.1.call-start = ((), (), s32[]{:S(2)}) async-start(), calls=%async_computation.45 | async-start | bytes 2621440 | tf_op jit(solution)/shard_map/reduce_scatter | solution.py:217
  1406.4 157.5 %reduce-scatter.44.cloned.1.call-start = ((), (), s32[]{:S(2)}) async-start(), calls=%async_computation.47 | async-start | bytes 2621440 | tf_op jit(solution)/shard_map/reduce_scatter | solution.py:294
  1566.4 117.2 %reduce-scatter.24.cloned.1.call-start = ((), (), s32[]{:S(2)}) async-start(), calls=%async_computation.24 | async-start | bytes 2621440 | tf_op jit(solution)/shard_map/reduce_scatter | solution.py:168
  1648.3 76.0 %all-gather.29.cloned.1.call-start = ((), (), s32[]{:S(2)}) async-start(), calls=%async_computation.25 | async-start | bytes 2621440 | tf_op jit(solution)/shard_map/all_gather | solution.py:191
  1688.9 79.0 %reduce-scatter.26.cloned.1.call-start = ((), (), s32[]{:S(2)}) async-start(), calls=%async_computation.26 | async-start | bytes 2621440 | tf_op jit(solution)/shard_map/reduce_scatter | solution.py:198
  1732.5 146.1 %all-reduce.3.cloned.1.call-start = ((), (), s32[]{:S(2)}) async-start(), calls=%async_computation.48 | async-start | bytes 131072 | tf_op jit(solution)/shard_map/psum | solution.py:409
  (161 other events, 3026.7 us)
Sparse Core Ops, SparseCore 0:
  16.6 38.0 all-gather.18
  101.5 35.1 reduce-scatter.15
  142.0 35.2 all-gather.20
  232.6 35.4 all-gather.22
  355.5 35.2 all-gather.24
  445.9 35.4 all-gather.46
  518.4 35.1 reduce-scatter.39
  557.3 35.3 all-gather.38
  594.5 35.3 all-gather.30
  711.0 35.2 all-gather.32
  748.2 35.2 all-gather.34
  835.2 35.2 all-gather.36
  960.5 35.1 reduce-scatter.31
  999.8 35.2 all-gather.40
  1037.2 35.2 all-gather.42
  1123.1 35.2 all-gather.44
  1282.8 35.2 all-gather.48
  1320.6 35.2 all-gather.50
  1406.5 35.2 all-gather.52
  1528.7 35.1 reduce-scatter.43
  1566.6 35.2 all-gather.26
  1689.0 35.2 all-gather.28
  1732.6 35.1 reduce-scatter.25
  1775.4 103.1 all-reduce.2
  (10 shorter events, 351.4 us)
where the time goes:
time: 1900 us; the launch traced here: 1890 us
  waiting for transfers between devices  1140 us (60%)
  matrix products  444 us (23%)
  other arithmetic  145 us (8%)
  local copies, waits for them, and re-layouts  113 us (6%)
  starting transfers between devices  22 us (1%)
    reduce_scatter x6, waiting for transfers between devices, attention_project(): lax.psum_scatter(jnp.einsum('srf,fd->srd', attended_b, w_out, preferred_e...  179 us
    all_gather x6, waiting for transfers between devices, mlp_pre(): lax.all_gather(normed_b, 'tensor', axis=0, tiled=True)  179 us
    all_gather x3, waiting for transfers between devices, forward_layer_step(): lax.all_gather(norm_rows, 'tensor', axis=0, tiled=True)  108 us
    all_gather x3, waiting for transfers between devices, attention_grad_heads(): lax.all_gather(grad_middle_b, 'tensor', axis=0, tiled=True)  106 us
    reduce_scatter x3, waiting for transfers between devices, mlp_back(): lax.psum_scatter(jnp.einsum('srf,df->srd', grad_pre, w_fc, preferred_elem...  106 us
    psum x1, waiting for transfers between devices, body(): lax.psum((gradient_totals[0], full_query, gradient_totals[2], full_value)...  105 us
    reduce_scatter x3, waiting for transfers between devices, backward_layer_step(): lax.psum_scatter((term + jnp.einsum('srk,dk->srd', thin_grad_value, a_val...  103 us
    all_gather x3, waiting for transfers between devices, mlp_back(): lax.all_gather(grad_mlp, 'tensor', axis=0, tiled=True)  94.5 us
  transfers between devices with their start and end apart: 38, of which 37 were waited for; matrix products, arithmetic and copies ran while one was open for 7% of the time, Pallas kernels for 0%

commit v1 on v0

--- a/solution.py
+++ b/solution.py
@@ -1,6 +1,10 @@
+import functools
+
 import jax
 import jax.numpy as jnp
 from jax import lax
+from jax.experimental import pallas as pl
+from jax.experimental.pallas import tpu as pltpu
 from jax.sharding import PartitionSpec as P
 
 HEAD_DIM = 64
@@ -419,6 +423,537 @@
     )
 
 
+ROUTE_AXES = ("section", "dp", "tensor")
+REACH = 512
+BF16 = jnp.bfloat16
+F32 = jnp.float32
+
+
+def route(planes, rule):
+    pairs = []
+    for c in range(2):
+        for z in range(planes):
+            for y in range(2):
+                for x in range(2):
+                    target = rule(c, z, y, x)
+                    if target is not None:
+                        tc, tz, ty, tx = target
+                        pairs.append(
+                            ((c * planes + z) * 4 + 2 * y + x, (tc * planes + tz) * 4 + 2 * ty + tx)
+                        )
+    return pairs
+
+
+def dot_nn(a, b):
+    return lax.dot_general(a, b, (((1,), (0,)), ((), ())), preferred_element_type=F32)
+
+
+def dot_nt(a, b):
+    return lax.dot_general(a, b, (((1,), (1,)), ((), ())), preferred_element_type=F32)
+
+
+def dot_tn(a, b):
+    return lax.dot_general(a, b, (((0,), (0,)), ((), ())), preferred_element_type=F32)
+
+
+def norm_stats(rows):
+    middle = jnp.mean(rows, axis=-1, keepdims=True)
+    centred = rows - middle
+    inverse = lax.rsqrt(jnp.mean(centred * centred, axis=-1, keepdims=True) + EPSILON)
+    return centred * inverse, inverse
+
+
+def key_span(i, block):
+    return max(0, i - REACH // block) * block, (i + 1) * block
+
+
+def allowed_keys(i, block, seg_col_ref, seg_row_ref):
+    low, high = key_span(i, block)
+    seg_q = seg_col_ref[i * block : (i + 1) * block, :]
+    seg_k = seg_row_ref[:, low:high]
+    places_q = i * block + lax.broadcasted_iota(jnp.int32, (block, high - low), 0)
+    places_k = low + lax.broadcasted_iota(jnp.int32, (block, high - low), 1)
+    return (seg_q == seg_k) & (places_k <= places_q)
+
+
+def head_lanes(rows, h):
+    lane = lax.broadcasted_iota(jnp.int32, (rows, 128), 1)
+    return (lane < HEAD_DIM) if h == 0 else (lane >= HEAD_DIM)
+
+
+def attention_forward_kernel(block, width, qkv_ref, seg_col_ref, seg_row_ref, out_ref):
+    length = qkv_ref.shape[0]
+    for i in range(length // block):
+        low, high = key_span(i, block)
+        rows = slice(i * block, (i + 1) * block)
+        allowed = allowed_keys(i, block, seg_col_ref, seg_row_ref)
+        for pair in range(width // 128):
+            lanes = slice(pair * 128, pair * 128 + 128)
+            queries = qkv_ref[rows, lanes] * BF16(HEAD_DIM**-0.5)
+            keys = qkv_ref[low:high, width + pair * 128 : width + pair * 128 + 128]
+            values = qkv_ref[low:high, 2 * width + pair * 128 : 2 * width + pair * 128 + 128]
+            parts = []
+            for h in range(2):
+                mine = jnp.where(head_lanes(block, h), queries, BF16(0))
+                scores = jnp.where(allowed, dot_nt(mine, keys), MASKED)
+                exponent = jnp.exp(scores - jnp.max(scores, axis=-1, keepdims=True))
+                total = jnp.sum(exponent, axis=-1, keepdims=True)
+                parts.append(dot_nn(exponent.astype(BF16), values) / total)
+            out_ref[rows, lanes] = jnp.where(head_lanes(block, 0), parts[0], parts[1]).astype(BF16)
+
+
+def attention_backward_kernel(
+    block, width, qkv_ref, grad_ref, seg_col_ref, seg_row_ref, out_ref, dk_ref, dv_ref
+):
+    length = qkv_ref.shape[0]
+    scale = HEAD_DIM**-0.5
+    for pair in range(width // 128):
+        lanes = slice(pair * 128, pair * 128 + 128)
+        lanes_k = slice(width + pair * 128, width + pair * 128 + 128)
+        lanes_v = slice(2 * width + pair * 128, 2 * width + pair * 128 + 128)
+        dk_ref[...] = jnp.zeros_like(dk_ref)
+        dv_ref[...] = jnp.zeros_like(dv_ref)
+        for i in range(length // block):
+            low, high = key_span(i, block)
+            rows = slice(i * block, (i + 1) * block)
+            allowed = allowed_keys(i, block, seg_col_ref, seg_row_ref)
+            queries = qkv_ref[rows, lanes] * BF16(scale)
+            keys = qkv_ref[low:high, lanes_k]
+            values = qkv_ref[low:high, lanes_v]
+            grads = grad_ref[rows, lanes]
+            parts = []
+            for h in range(2):
+                mine = jnp.where(head_lanes(block, h), queries, BF16(0))
+                grad = jnp.where(head_lanes(block, h), grads, BF16(0))
+                scores = jnp.where(allowed, dot_nt(mine, keys), MASKED)
+                exponent = jnp.exp(scores - jnp.max(scores, axis=-1, keepdims=True))
+                soft = exponent * (1.0 / jnp.sum(exponent, axis=-1, keepdims=True))
+                grad_soft = dot_nt(grad, values)
+                weighted = soft * grad_soft
+                grad_scores = (
+                    weighted - soft * jnp.sum(weighted, axis=-1, keepdims=True)
+                ).astype(BF16)
+                parts.append(dot_nn(grad_scores, keys))
+                dk_ref[low:high, :] += dot_tn(grad_scores, mine)
+                dv_ref[low:high, :] += dot_tn(soft.astype(BF16), grad)
+            out_ref[rows, lanes] = (
+                jnp.where(head_lanes(block, 0), parts[0], parts[1]) * scale
+            ).astype(BF16)
+        out_ref[:, lanes_k] = dk_ref[...].astype(BF16)
+        out_ref[:, lanes_v] = dv_ref[...].astype(BF16)
+
+
+SLOTS = 3
+
+
+def weight_stream(core_ref, own_refs, twin_refs, fc_buf, proj_buf, sems, chunk):
+    width = own_refs[0].shape[0]
+    per = width // chunk
+    first = core_ref[0] == 0
+
+    def copies(k, slot, flag):
+        array = k // per
+        cut = pl.ds((k % per) * chunk, chunk)
+        fc_from, proj_from = (own_refs, twin_refs) if flag else (twin_refs, own_refs)
+        return (
+            pltpu.make_async_copy(fc_from[array].at[:, cut], fc_buf.at[slot], sems.at[0, slot]),
+            pltpu.make_async_copy(proj_from[array].at[cut, :], proj_buf.at[slot], sems.at[1, slot]),
+        )
+
+    def start(k):
+        @pl.when(first)
+        def _():
+            for copy in copies(k, k % SLOTS, True):
+                copy.start()
+
+        @pl.when(jnp.logical_not(first))
+        def _():
+            for copy in copies(k, k % SLOTS, False):
+                copy.start()
+
+    def wait(k):
+        for copy in copies(k, k % SLOTS, True):
+            copy.wait()
+
+    return start, wait, per * len(own_refs)
+
+
+def mlp_forward_kernel(
+    chunk, arrays, core_ref, x_ref, o_ref, w_out_ref, gain_ref, *refs
+):
+    own_refs, twin_refs = refs[:arrays], refs[arrays : 2 * arrays]
+    middle_ref, pre_ref, act_ref, fc_buf, proj_buf, sems = refs[2 * arrays :]
+    start, wait, steps = weight_stream(core_ref, own_refs, twin_refs, fc_buf, proj_buf, sems, chunk)
+    for k in range(min(SLOTS - 1, steps)):
+        start(k)
+    middle = x_ref[...].astype(F32) + dot_nn(o_ref[...], w_out_ref[...])
+    middle_ref[...] = middle
+    unit, _ = norm_stats(middle)
+    normed = (unit * gain_ref[...]).astype(BF16)
+    total = middle
+    for k in range(steps):
+        wait(k)
+        if k + SLOTS - 1 < steps:
+            start(k + SLOTS - 1)
+        pre = dot_nn(normed, fc_buf[k % SLOTS])
+        pre_ref[:, k * chunk : (k + 1) * chunk] = pre.astype(BF16)
+        hidden = gelu_tanh(pre).astype(BF16)
+        total = total + dot_nn(hidden, proj_buf[k % SLOTS])
+    act_ref[...] = total.astype(BF16)
+
+
+def mlp_backward_kernel(
+    chunk, arrays, core_ref, up_ref, middle_ref, pre_ref, w_out_ref, gain_ref, *refs
+):
+    own_refs, twin_refs = refs[:arrays], refs[arrays : 2 * arrays]
+    grad_ref, heads_ref, fc_buf, proj_buf, sems = refs[2 * arrays :]
+    start, wait, steps = weight_stream(core_ref, own_refs, twin_refs, fc_buf, proj_buf, sems, chunk)
+    for k in range(min(SLOTS - 1, steps)):
+        start(k)
+    upstream = up_ref[...]
+    grad_norm = None
+    for k in range(steps):
+        wait(k)
+        if k + SLOTS - 1 < steps:
+            start(k + SLOTS - 1)
+        grad_hidden = dot_nt(upstream, proj_buf[k % SLOTS])
+        pre = pre_ref[:, k * chunk : (k + 1) * chunk].astype(F32)
+        square = pre * pre
+        bent = jnp.tanh(TANH_SCALE * (pre + CUBIC_TERM * square * pre))
+        slope = 0.5 * (1.0 + bent) + (0.5 * TANH_SCALE) * pre * (1.0 - bent * bent) * (
+            1.0 + (3.0 * CUBIC_TERM) * square
+        )
+        term = dot_nt((grad_hidden * slope).astype(BF16), fc_buf[k % SLOTS])
+        grad_norm = term if grad_norm is None else grad_norm + term
+    unit, inverse = norm_stats(middle_ref[...])
+    grad_middle = upstream.astype(F32) + normalize_back(grad_norm, unit, inverse, gain_ref[...])
+    grad_ref[...] = grad_middle
+    heads_ref[...] = dot_nt(grad_middle.astype(BF16), w_out_ref[...]).astype(BF16)
+
+
+def in_vmem():
+    return pl.BlockSpec(memory_space=pltpu.VMEM)
+
+
+def kernel_params():
+    return pltpu.CompilerParams(vmem_limit_bytes=48 * 1024 * 1024)
+
+
+def attend_forward(qkv, seg_col, seg_row, block):
+    length, wide = qkv.shape
+    width = wide // 3
+    return pl.pallas_call(
+        functools.partial(attention_forward_kernel, block, width),
+        out_shape=jax.ShapeDtypeStruct((length, width), BF16),
+        in_specs=[in_vmem()] * 3,
+        out_specs=in_vmem(),
+        compiler_params=kernel_params(),
+        cost_estimate=pl.CostEstimate(
+            flops=6_000_000_000, bytes_accessed=2_000_000, transcendentals=0
+        ),
+    )(qkv, seg_col, seg_row)
+
+
+def attend_backward(qkv, grads, seg_col, seg_row, block):
+    length, wide = qkv.shape
+    width = wide // 3
+    return pl.pallas_call(
+        functools.partial(attention_backward_kernel, block, width),
+        out_shape=jax.ShapeDtypeStruct((length, wide), BF16),
+        in_specs=[in_vmem()] * 4,
+        out_specs=in_vmem(),
+        scratch_shapes=[pltpu.VMEM((length, 128), F32), pltpu.VMEM((length, 128), F32)],
+        compiler_params=kernel_params(),
+        cost_estimate=pl.CostEstimate(
+            flops=12_000_000_000, bytes_accessed=4_000_000, transcendentals=0
+        ),
+    )(qkv, grads, seg_col, seg_row)
+
+
+def mlp_call(kernel, core, given, weights, outs, chunk):
+    own, twin = weights
+    anywhere = pl.BlockSpec(memory_space=pl.ANY)
+    width = own[0].shape[1]
+    return pl.pallas_call(
+        functools.partial(kernel, chunk, len(own)),
+        out_shape=outs,
+        in_specs=[pl.BlockSpec(memory_space=pltpu.SMEM)]
+        + [in_vmem()] * len(given)
+        + [anywhere] * (2 * len(own)),
+        out_specs=[in_vmem()] * len(outs),
+        scratch_shapes=[
+            pltpu.VMEM((SLOTS, width, chunk), BF16),
+            pltpu.VMEM((SLOTS, chunk, width), BF16),
+            pltpu.SemaphoreType.DMA((2, SLOTS)),
+        ],
+        compiler_params=kernel_params(),
+        cost_estimate=pl.CostEstimate(
+            flops=5_000_000_000, bytes_accessed=20_000_000, transcendentals=0
+        ),
+    )(core, *given, *own, *twin)
+
+
+def fast_body(
+    planes,
+    inputs,
+    segments,
+    cotangent,
+    gain_attn,
+    joint_projection_weight,
+    query_down_factor,
+    query_up_factor,
+    value_down_factor,
+    value_up_factor,
+    w_out,
+    gain_mlp,
+    w_fc,
+    w_proj,
+):
+    core = lax.axis_index("section")
+    place = lax.axis_index("tensor")
+    y, x = place // 2, place % 2
+    block, _, model = inputs.shape
+    width = joint_projection_weight.shape[3]
+    rank = query_down_factor.shape[2]
+    factor = 32.0 / rank
+    core_0, y_0, x_0 = core == 0, y == 0, x == 0
+
+    def sent(value, rule):
+        return lax.ppermute(value, ROUTE_AXES, route(planes, rule))
+
+    def c_flip(value):
+        return sent(value, lambda c, z, y, x: (1 - c, z, y, x))
+
+    def y_flip(value):
+        return sent(value, lambda c, z, y, x: (c, z, 1 - y, x))
+
+    def x_flip(value):
+        return sent(value, lambda c, z, y, x: (c, z, y, 1 - x))
+
+    def z_flip(value, bit):
+        return sent(value, lambda c, z, y, x: (c, z ^ bit, y, x))
+
+    def in_order(first, one, other):
+        return jnp.concatenate(
+            [jnp.where(first, one, other), jnp.where(first, other, one)], axis=0
+        )
+
+    def both_layers(own):
+        twin = c_flip(own)
+        return jnp.where(core_0, own, twin), jnp.where(core_0, twin, own)
+
+    def to_row(array):
+        mine = jnp.where(x_0, array[:, 0], array[:, 1])
+        other = jnp.where(x_0, array[:, 1], array[:, 0])
+        came = sent(other, lambda c, z, y, x: (c, z, y, 1 - x) if c == x else None)
+        return jnp.where(core == x, mine, came)
+
+    layer_input = to_row(inputs)
+    segment_row = jnp.where(x_0, segments[0], segments[1])
+    seg_col, seg_row = segment_row[:, None], segment_row[None, :]
+    small = jnp.concatenate(
+        [
+            gain_attn,
+            gain_mlp,
+            query_down_factor[0].T.astype(F32),
+            value_down_factor[0].T.astype(F32),
+        ],
+        axis=0,
+    )
+    smalls = both_layers(small)
+    gains_a = [s[0:1] for s in smalls]
+    gains_m = [s[1:2] for s in smalls]
+    downs = [s[2 : 2 + 2 * rank].T.astype(BF16) for s in smalls]
+
+    blank = jnp.zeros((rank, width), BF16)
+    ups_own = jnp.concatenate(
+        [
+            jnp.concatenate([query_up_factor[0], blank, blank], axis=1),
+            jnp.concatenate([blank, blank, value_up_factor[0]], axis=1),
+        ],
+        axis=0,
+    )
+    packed = jnp.concatenate(
+        [joint_projection_weight[0].reshape(model, 3 * width), ups_own, jnp.zeros_like(ups_own)],
+        axis=0,
+    )
+    heads_weights = []
+    for own in both_layers(packed):
+        came = sent(own, lambda c, z, y, x: (c, z, y, 1 - x) if c == x else None)
+        heads_weights.append(jnp.where(core == x, own, came))
+    w_qkv = [w[:model] for w in heads_weights]
+    ups = [w[model : model + 2 * rank] for w in heads_weights]
+    w_outs = both_layers(lax.all_gather(w_out[0], "tensor", axis=0, tiled=True))
+
+    twin = c_flip(jnp.where(core_0, w_proj[0], w_fc[0]))
+    kept = jnp.where(core_0, w_fc[0], w_proj[0])
+    half = model // 2
+    ff_weights = []
+    before = None
+    for own in (jnp.where(core_0, kept, twin), jnp.where(core_0, twin, kept)):
+        if before is not None:
+            own, _ = lax.optimization_barrier((own, before))
+        over_x = x_flip(own)
+        over_y = y_flip(own)
+        diagonal = jnp.concatenate([y_flip(over_x[:half]), x_flip(over_y[half:])], axis=0)
+        arrays = (own, over_x, over_y, diagonal)
+        ff_weights.append((arrays, tuple(c_flip(a) for a in arrays)))
+        before = over_y
+    core_id = core.astype(jnp.int32).reshape(1)
+
+    def gathered(own):
+        over_y = y_flip(own)
+        chip = in_order(core_0, own, c_flip(own))
+        across = in_order(core_0, over_y, c_flip(over_y))
+        return in_order(y_0, chip, across)
+
+    def split(array):
+        upper, lower = array[: 2 * block], array[2 * block :]
+        return jnp.where(y_0, upper, lower), jnp.where(y_0, lower, upper)
+
+    def mine_and_twins(pair):
+        upper, lower = pair[:block], pair[block:]
+        return jnp.where(core_0, upper, lower), jnp.where(core_0, lower, upper)
+
+    def heads_to_slots(attended):
+        here, there = split(attended)
+        here_mine, here_twin = mine_and_twins(here)
+        there_mine, there_twin = mine_and_twins(there)
+        came = c_flip(jnp.concatenate([here_twin, there_twin], axis=0))
+        here_all = in_columns(core_0, here_mine, came[:block])
+        there_all = in_columns(core_0, there_mine, came[block:])
+        return in_columns(y_0, here_all, y_flip(there_all))
+
+    def in_columns(first, one, other):
+        return jnp.concatenate(
+            [jnp.where(first, one, other), jnp.where(first, other, one)], axis=1
+        )
+
+    def slots_to_heads(slots):
+        left, right = slots[:, : 2 * width], slots[:, 2 * width :]
+        across = y_flip(jnp.where(y_0, right, left))
+        pair = jnp.concatenate([jnp.where(y_0, left, right), across], axis=0)
+        left, right = pair[:, :width], pair[:, width:]
+        came = c_flip(jnp.where(core_0, right, left))
+        own = jnp.where(core_0, left, right)
+        here = in_order(core_0, own[:block], came[:block])
+        there = in_order(core_0, own[block:], came[block:])
+        return in_order(y_0, here, there)
+
+    kept_layers = []
+    acts = []
+    for layer in range(2):
+        unit, inverse = norm_stats(layer_input.astype(F32))
+        rows = gathered((unit * gains_a[layer]).astype(BF16))
+        thin = dot_nn(rows, downs[layer])
+        extra = factor * dot_nn(thin.astype(BF16), ups[layer])
+        qkv = (dot_nn(rows, w_qkv[layer]) + extra).astype(BF16)
+        attended = heads_to_slots(attend_forward(qkv, seg_col, seg_row, block))
+        middle, pre_act, act = mlp_call(
+            mlp_forward_kernel,
+            core_id,
+            (layer_input, attended, w_outs[layer], gains_m[layer]),
+            ff_weights[layer],
+            (
+                jax.ShapeDtypeStruct((block, model), F32),
+                jax.ShapeDtypeStruct((block, 4 * model), BF16),
+                jax.ShapeDtypeStruct((block, model), BF16),
+            ),
+            512,
+        )
+        kept_layers.append((layer_input, rows, thin, qkv, middle, pre_act))
+        acts.append(act)
+        layer_input = act
+
+    grads_in = [None, None]
+    sums = [None, None]
+    upstream = to_row(cotangent)
+    for layer in (1, 0):
+        layer_input, rows, thin, qkv, middle, pre_act = kept_layers[layer]
+        grad_middle, grad_heads = mlp_call(
+            mlp_backward_kernel,
+            core_id,
+            (upstream, middle, pre_act, w_outs[layer], gains_m[layer]),
+            ff_weights[layer],
+            (
+                jax.ShapeDtypeStruct((block, model), F32),
+                jax.ShapeDtypeStruct((block, model), BF16),
+            ),
+            512,
+        )
+        grad_qkv = attend_backward(qkv, slots_to_heads(grad_heads), seg_col, seg_row, block)
+        thin_grad = factor * dot_nt(grad_qkv, ups[layer])
+        thin_grad_b = thin_grad.astype(BF16)
+        term = dot_nt(grad_qkv, w_qkv[layer]) + dot_nt(thin_grad_b, downs[layer])
+        here, there = split(term)
+        here_mine, here_twin = mine_and_twins(here)
+        there_mine, there_twin = mine_and_twins(there)
+        came = c_flip(jnp.concatenate([here_twin, there_twin], axis=0).astype(BF16)).astype(F32)
+        across = y_flip((there_mine + came[block:]).astype(BF16)).astype(F32)
+        grad_norm = here_mine + came[:block] + across
+        unit, inverse = norm_stats(layer_input.astype(F32))
+        upstream = (
+            grad_middle + normalize_back(grad_norm, unit, inverse, gains_a[layer])
+        ).astype(BF16)
+        grads_in[layer] = upstream
+        grad_down = dot_tn(thin_grad_b, rows)
+        thin_b = thin.astype(BF16)
+        spread = [
+            lax.dynamic_update_slice_in_dim(
+                jnp.zeros((rank, model), F32), factor * dot_tn(one, grads), (2 * y + core) * width, 1
+            )
+            for one, grads in (
+                (thin_b[:, :rank], grad_qkv[:, :width]),
+                (thin_b[:, rank:], grad_qkv[:, 2 * width :]),
+            )
+        ]
+        total = jnp.concatenate([grad_down, *spread], axis=0)
+        total = total + c_flip(total)
+        total = total + x_flip(total)
+        total = total + y_flip(total)
+        bit = 1
+        while bit < planes:
+            total = total + z_flip(total, bit)
+            bit *= 2
+        sums[layer] = total
+
+    def placed(pair):
+        same, other = [], []
+        for layer in range(2):
+            same.append(
+                sent(pair[layer], lambda c, z, y, x: (layer, z, y, x) if c == x else None)
+            )
+            other.append(
+                sent(pair[layer], lambda c, z, y, x: (layer, z, y, 1 - x) if c != x else None)
+            )
+        same = jnp.where(core_0, same[0], same[1])
+        other = jnp.where(core_0, other[0], other[1])
+        return jnp.stack([jnp.where(x_0, same, other), jnp.where(x_0, other, same)], axis=1)[None]
+
+    total = jnp.where(core_0, sums[0], sums[1])
+    return (
+        placed(acts),
+        placed(grads_in),
+        total[:rank].T[None],
+        total[2 * rank : 3 * rank][None],
+        total[rank : 2 * rank].T[None],
+        total[3 * rank :][None],
+    )
+
+
+def fits_fast(mesh, shapes):
+    planes = mesh.shape["dp"]
+    return (
+        mesh.shape["section"] == 2
+        and mesh.shape["tensor"] == 4
+        and planes & (planes - 1) == 0
+        and shapes[0][1] == 2 * planes
+        and shapes[0][0] % 1024 == 0
+        and shapes[0][0] // 4 <= REACH
+        and REACH % (shapes[0][0] // 4) == 0
+    )
+
+
 def solution(mesh):
     placed = (
         P("tensor", "dp", None),
@@ -435,8 +970,15 @@
         P("section", None, "tensor"),
         P("section", "tensor", None),
     )
-    return jax.shard_map(
-        body,
+    def choose(*args):
+        picked = body
+        if fits_fast(mesh, [a.shape for a in args]):
+            picked = functools.partial(fast_body, mesh.shape["dp"])
+        return mapped(picked)(*args)
+
+    def mapped(picked):
+      return jax.shard_map(
+        picked,
         mesh=mesh,
         in_specs=placed,
         out_specs=(
@@ -449,3 +991,5 @@
         ),
         check_vma=False,
     )
+
+    return choose

time: 1900 us -> 506 us (0.27)
  waiting for transfers between devices: 1140 us -> 228 us
  matrix products: 444 us -> 14.3 us
  other arithmetic: 145 us -> 34.6 us
  Pallas kernels: 0 us -> 81.4 us
  local copies, waits for them, and re-layouts: 113 us -> 60.9 us
  starting transfers between devices: 22 us -> 64 us
    all_gather x18 -> x1, waiting for transfers between devices: 558 us -> 0.02 us  [fast_body(): w_outs = both_layers(lax.all_gather(w_out[0], 'tensor', axis=0, tiled=True))]
    reduce_scatter x15 -> x0, waiting for transfers between devices: 467 us -> none  [the longest x6 179 us: attention_project(): lax.psum_scatter(jnp.einsum('srf,fd->srd', attended_b, w_out, preferred_e...]
    dot_general x123 -> x18, matrix products: 398 us -> 14.3 us  [the longest x6 6.56 us: dot_nt(): lax.dot_general(a, b, (((1,), (1,)), ((), ())), preferred_element_type=F32)]
    ppermute x4 -> x60, waiting for transfers between devices: 6.38 us -> 228 us  [sent(): return lax.ppermute(value, ROUTE_AXES, route(planes, rule))]
    psum x1 -> x0, waiting for transfers between devices: 105 us -> none  [body(): lax.psum((gradient_totals[0], full_query, gradient_totals[2], full_value)...]
    pallas_call x0 -> x8, Pallas kernels: none -> 81.4 us  [the longest x4 45 us: mlp_call(): pl.pallas_call(functools.partial(kernel, chunk, len(own)), out_shape=outs...]
    ppermute x4 -> x60, starting transfers between devices: 7.66 us -> 64 us  [sent(): return lax.ppermute(value, ROUTE_AXES, route(planes, rule))]
    another operation x29 -> x4, local copies, waits for them, and re-layouts: 45.4 us -> 0.01 us  [choose(): return mapped(picked)(*args)]
  transfers between devices with their start and end apart: 38 -> 61, of which waited for: 37 -> 24; matrix products, arithmetic and copies ran while one was open for 7% -> 16% of each run, Pallas kernels for 0% -> 7%
where the time goes in v1:
time: 506 us; the launch traced here: 499 us
  waiting for transfers between devices  228 us (45%)
  Pallas kernels  81.4 us (16%)
  starting transfers between devices  64 us (13%)
  local copies, waits for them, and re-layouts  60.9 us (12%)
  other arithmetic  34.6 us (7%)
  between operations  16 us (3%)
  matrix products  14.3 us (3%)
    ppermute x60, waiting for transfers between devices, sent(): return lax.ppermute(value, ROUTE_AXES, route(planes, rule))  228 us
    ppermute x60, starting transfers between devices, sent(): return lax.ppermute(value, ROUTE_AXES, route(planes, rule))  64 us
    pallas_call x4, Pallas kernels, mlp_call(): pl.pallas_call(functools.partial(kernel, chunk, len(own)), out_shape=outs...  45 us
    pallas_call x2, Pallas kernels, attend_backward(): pl.pallas_call(functools.partial(attention_backward_kernel, block, width)...  24.8 us
    unnamed x111, local copies, waits for them, and re-layouts  23.8 us
    ppermute x3, local copies, waits for them, and re-layouts, sent(): return lax.ppermute(value, ROUTE_AXES, route(planes, rule))  11.8 us
    pallas_call x2, Pallas kernels, attend_forward(): pl.pallas_call(functools.partial(attention_forward_kernel, block, width),...  11.6 us
  transfers between devices with their start and end apart: 61, of which 24 were waited for; matrix products, arithmetic and copies ran while one was open for 16% of the time, Pallas kernels for 7%

profile of v1, /device:TPU:0, one launch (start us, length us, event | category | flops | bytes accessed | tf_op | source)
XLA Modules:
  0.0 498.8 jit_solution(12405051369472805700)
XLA Ops:
  12.7 5.0 %collective-permute-start = (bf16[256,1024]{1,0:T(8,128)(2,1)}, bf16[256,1024]{1,0:T(8,128)(2,1)S(1)}, u32[]{:S(2)}, u32[]{:S(2)}) collective-permute-start(bf16[256,1024]{1,0:T(8,128)(2,1)} %select_bitcast_fusion.6), channel_id=1, source_target_pairs={{0,1},{2,3},{4,5},{6,7},{8,9},{10,11},{12,13},{14,15},{17,16},{19,... | collective-permute-start | bytes 1572872 | tf_op jit(solution)/shard_map/ppermute | solution.py:722
  33.9 15.8 %collective-permute-done.3 = bf16[256,1024]{1,0:T(8,128)(2,1)S(1)} collective-permute-done((bf16[256,1024]{1,0:T(8,128)(2,1)}, bf16[256,1024]{1,0:T(8,128)(2,1)S(1)}, u32[]{:S(2)}, u32[]{:S(2)}) %collective-permute-start.3) | collective-permute-done | bytes 524320 | tf_op jit(solution)/shard_map/ppermute | solution.py:722
  91.0 5.7 %shard_map.172 = bf16[1024,256]{1,0:T(8,128)(2,1)S(1)} custom-call(bf16[1024,768]{1,0:T(8,128)(2,1)S(1)} %add_convert_fusion.1.qkv_ref, s32[1024,1]{1,0:T(8,128)S(1)} %copy.55.seg_col_ref, s32[1,1024]{1,0:T(1,128)S(1)} %broadcast_select_fusion.69.seg_row_ref), custom_call_target="tpu_custom_call" | custom-call | flops 6000000000 | bytes 2000000 | tf_op jit(solution)/shard_map/pallas_call | solution.py:645
  96.7 23.6 %collective-permute-done.12.refs_2_ = bf16[1024,1024]{1,0:T(8,128)(2,1)} collective-permute-done((bf16[1024,1024]{1,0:T(8,128)(2,1)}, bf16[1024,1024]{1,0:T(8,128)(2,1)}, u32[]{:S(2)}, u32[]{:S(2)}) %collective-permute-start.12) | collective-permute-done | bytes 2097184 | tf_op jit(solution)/shard_map/ppermute | solution.py:722
  120.6 38.6 %collective-permute-done.11.refs_1_ = bf16[1024,1024]{1,0:T(8,128)(2,1)} collective-permute-done((bf16[1024,1024]{1,0:T(8,128)(2,1)}, bf16[1024,1024]{1,0:T(8,128)(2,1)}, u32[]{:S(2)}, u32[]{:S(2)}) %collective-permute-start.11) | collective-permute-done | bytes 2097184 | tf_op jit(solution)/shard_map/ppermute | solution.py:722
  167.5 18.0 %collective-permute-done.13 = bf16[512,1024]{1,0:T(8,128)(2,1)S(1)} collective-permute-done((bf16[512,1024]{1,0:T(8,128)(2,1)S(1)}, bf16[512,1024]{1,0:T(8,128)(2,1)S(1)}, u32[]{:S(2)}, u32[]{:S(2)}) %collective-permute-start.13) | collective-permute-done | bytes 1048608 | tf_op jit(solution)/shard_map/ppermute | solution.py:722
  188.9 22.3 %collective-permute-done.14 = bf16[512,1024]{1,0:T(8,128)(2,1)S(1)} collective-permute-done((bf16[512,1024]{1,0:T(8,128)(2,1)S(1)}, bf16[512,1024]{1,0:T(8,128)(2,1)S(1)}, u32[]{:S(2)}, u32[]{:S(2)}) %collective-permute-start.14) | collective-permute-done | bytes 1048608 | tf_op jit(solution)/shard_map/ppermute | solution.py:722
  218.3 4.2 copy.58
  229.3 29.7 %collective-permute-done.27.refs_2_ = bf16[1024,1024]{1,0:T(8,128)(2,1)} collective-permute-done((bf16[1024,1024]{1,0:T(8,128)(2,1)}, bf16[1024,1024]{1,0:T(8,128)(2,1)}, u32[]{:S(2)}, u32[]{:S(2)}) %collective-permute-start.27) | collective-permute-done | bytes 2097184 | tf_op jit(solution)/shard_map/ppermute | solution.py:722
  264.6 10.9 %shard_map.173 = (f32[256,1024]{1,0:T(8,128)S(1)}, bf16[256,4096]{1,0:T(8,128)(2,1)S(1)}, bf16[256,1024]{1,0:T(8,128)(2,1)S(1)}) custom-call(s32[1]{0:T(128)} %bitcast.core_ref, bf16[256,1024]{1,0:T(8,128)(2,1)S(1)} %get-tuple-element.53.x_ref, bf16[256,1024]{1,0:T(8,128)(2,1)S(1)} %pad_maximum_fusion.14.o_ref, ...), custom_call_target="tpu_custom_call" | custom-call | flops 5000000000 | bytes 20000000 | tf_op jit(solution)/shard_map/pallas_call | solution.py:677
  278.5 6.6 %collective-permute-done.28 = bf16[512,1024]{1,0:T(8,128)(2,1)} collective-permute-done((bf16[512,1024]{1,0:T(8,128)(2,1)S(1)}, bf16[512,1024]{1,0:T(8,128)(2,1)}, u32[]{:S(2)}, u32[]{:S(2)}) %collective-permute-start.28) | collective-permute-done | bytes 1048608 | tf_op jit(solution)/shard_map/ppermute | solution.py:722
  285.1 11.0 %collective-permute-done.21 = bf16[256,1024]{1,0:T(8,128)(2,1)S(1)} collective-permute-done((bf16[256,1024]{1,0:T(8,128)(2,1)S(1)}, bf16[256,1024]{1,0:T(8,128)(2,1)S(1)}, u32[]{:S(2)}, u32[]{:S(2)}) %collective-permute-start.21) | collective-permute-done | bytes 524320 | tf_op jit(solution)/shard_map/ppermute | solution.py:722
  303.2 5.9 %shard_map.174 = bf16[1024,256]{1,0:T(8,128)(2,1)S(1)} custom-call(bf16[1024,768]{1,0:T(8,128)(2,1)S(1)} %add_convert_fusion.qkv_ref, s32[1024,1]{1,0:T(8,128)S(1)} %copy.55.seg_col_ref, s32[1,1024]{1,0:T(1,128)S(1)} %broadcast_select_fusion.69.seg_row_ref), custom_call_target="tpu_custom_call" | custom-call | flops 6000000000 | bytes 2000000 | tf_op jit(solution)/shard_map/pallas_call | solution.py:645
  312.3 6.6 %collective-permute-done.37 = bf16[256,1024]{1,0:T(8,128)(2,1)S(1)} collective-permute-done((bf16[256,1024]{1,0:T(8,128)(2,1)S(1)}, bf16[256,1024]{1,0:T(8,128)(2,1)S(1)}, u32[]{:S(2)}, u32[]{:S(2)}) %collective-permute-start.37) | collective-permute-done | bytes 524320 | tf_op jit(solution)/shard_map/ppermute | solution.py:722
  320.8 6.2 %collective-permute-done.25 = bf16[256,512]{1,0:T(8,128)(2,1)S(1)} collective-permute-done((bf16[256,512]{1,0:T(8,128)(2,1)S(1)}, bf16[256,512]{1,0:T(8,128)(2,1)S(1)}, u32[]{:S(2)}, u32[]{:S(2)}) %collective-permute-start.25) | collective-permute-done | bytes 262176 | tf_op jit(solution)/shard_map/ppermute | solution.py:722
  329.8 10.8 %shard_map.175 = (f32[256,1024]{1,0:T(8,128)S(1)}, bf16[256,4096]{1,0:T(8,128)(2,1)S(1)}, bf16[256,1024]{1,0:T(8,128)(2,1)S(1)}) custom-call(s32[1]{0:T(128)} %bitcast.core_ref, bf16[256,1024]{1,0:T(8,128)(2,1)S(1)} %get-tuple-element.17.x_ref, bf16[256,1024]{1,0:T(8,128)(2,1)S(1)} %pad_maximum_fusion.15.o_ref, ...), custom_call_target="tpu_custom_call" | custom-call | flops 5000000000 | bytes 20000000 | tf_op jit(solution)/shard_map/pallas_call | solution.py:677
  340.6 12.0 %shard_map.176 = (f32[256,1024]{1,0:T(8,128)S(1)}, bf16[256,1024]{1,0:T(8,128)(2,1)S(1)}) custom-call(s32[1]{0:T(128)} %bitcast.core_ref, bf16[256,1024]{1,0:T(8,128)(2,1)S(1)} %bitcast_select_fusion.2.up_ref, f32[256,1024]{1,0:T(8,128)S(1)} %get-tuple-element.20.middle_ref, bf16[256,4096]{1,0:T(8,128)(2,1)S(1)} %get-tuple-element.21.pre_ref, ...), custom_call_target="tpu_custom_call" | custom-call | flops 5000000000 | bytes 20000000 | tf_op jit(solution)/shard_map/pallas_call | solution.py:677
  354.3 7.6 %collective-permute-done.38 = bf16[256,512]{1,0:T(8,128)(2,1)S(1)} collective-permute-done((bf16[256,512]{1,0:T(8,128)(2,1)S(1)}, bf16[256,512]{1,0:T(8,128)(2,1)S(1)}, u32[]{:S(2)}, u32[]{:S(2)}) %collective-permute-start.38) | collective-permute-done | bytes 262176 | tf_op jit(solution)/shard_map/ppermute | solution.py:722
  363.8 12.3 %shard_map.177 = bf16[1024,768]{1,0:T(8,128)(2,1)S(1)} custom-call(bf16[1024,768]{1,0:T(8,128)(2,1)S(1)} %add_convert_fusion.qkv_ref, bf16[1024,256]{1,0:T(8,128)(2,1)S(1)} %pad_maximum_fusion.16.grad_ref, s32[1024,1]{1,0:T(8,128)S(1)} %copy.55.seg_col_ref, s32[1,1024]{1,0:T(1,128)S(1)} %broadcast_select_fusion.69.seg_row_ref), custom_call_target="tpu_custom_call" | custom-call | flops 12000000000 | bytes 4000000 | tf_op jit(solution)/shard_map/pallas_call | solution.py:660
  387.5 12.7 %collective-permute-done.41 = bf16[256,1024]{1,0:T(8,128)(2,1)} collective-permute-done((bf16[256,1024]{1,0:T(8,128)(2,1)}, bf16[256,1024]{1,0:T(8,128)(2,1)}, u32[]{:S(2)}, u32[]{:S(2)}) %collective-permute-start.41) | collective-permute-done | bytes 524320 | tf_op jit(solution)/shard_map/ppermute | solution.py:722
  404.6 11.4 %shard_map.178 = (f32[256,1024]{1,0:T(8,128)S(1)}, bf16[256,1024]{1,0:T(8,128)(2,1)S(1)}) custom-call(s32[1]{0:T(128)} %bitcast.core_ref, bf16[256,1024]{1,0:T(8,128)(2,1)S(1)} %fusion.25.up_ref, f32[256,1024]{1,0:T(8,128)S(1)} %copy-done.5, bf16[256,4096]{1,0:T(8,128)(2,1)S(1)} %copy-done.1, bf16[1024,1024]{1,0:T(8,128)(2,1)} %get-tuple-element.61.w_out_ref, ...), custom_call_target="tpu_custom_call" | custom-call | flops 5000000000 | bytes 20000000 | tf_op jit(solution)/shard_map/pallas_call | solution.py:677
  418.1 5.6 %collective-permute-done.42 = bf16[256,512]{1,0:T(8,128)(2,1)S(1)} collective-permute-done((bf16[256,512]{1,0:T(8,128)(2,1)S(1)}, bf16[256,512]{1,0:T(8,128)(2,1)S(1)}, u32[]{:S(2)}, u32[]{:S(2)}) %collective-permute-start.42) | collective-permute-done | bytes 262176 | tf_op jit(solution)/shard_map/ppermute | solution.py:722
  425.7 12.5 %shard_map.179 = bf16[1024,768]{1,0:T(8,128)(2,1)S(1)} custom-call(bf16[1024,768]{1,0:T(8,128)(2,1)S(1)} %copy-done.9, bf16[1024,256]{1,0:T(8,128)(2,1)S(1)} %pad_maximum_fusion.17.grad_ref, s32[1024,1]{1,0:T(8,128)S(1)} %copy.55.seg_col_ref, s32[1,1024]{1,0:T(1,128)S(1)} %broadcast_select_fusion.69.seg_row_ref), custom_call_target="tpu_custom_call" | custom-call | flops 12000000000 | bytes 4000000 | tf_op jit(solution)/shard_map/pallas_call | solution.py:660
  481.9 7.3 %collective-permute-done.48 = bf16[256,1024]{1,0:T(8,128)(2,1)S(1)} collective-permute-done((bf16[256,1024]{1,0:T(8,128)(2,1)S(1)}, bf16[256,1024]{1,0:T(8,128)(2,1)S(1)}, u32[]{:S(2)}, u32[]{:S(2)}) %collective-permute-start.48) | collective-permute-done | bytes 524320 | tf_op jit(solution)/shard_map/ppermute | solution.py:722
  (353 shorter events, 180.7 us)
Async XLA Ops:
  7.2 74.1 %all-gather.3.cloned.1.call-start = ((), (), s32[]{:S(2)}) async-start(), calls=%async_computation | async-start | bytes 2621440 | tf_op jit(solution)/shard_map/all_gather | solution.py:786
  25.1 24.7 %collective-permute-start.5 = (bf16[1040,768]{1,0:T(8,128)(2,1)}, bf16[1040,768]{1,0:T(8,128)(2,1)}, u32[]{:S(2)}, u32[]{:S(2)}) collective-permute-start(bf16[1040,768]{1,0:T(8,128)(2,1)} %copy.51), channel_id=1, source_target_pairs={{0,16},{1,17},{2,18},{3,19},{4,20},{5,21},{6,22},{7,23},{8,24},{9,... | collective-permute-start | bytes 4792328 | tf_op jit(solution)/shard_map/ppermute | solution.py:722
  33.1 34.2 %collective-permute-start.10 = (bf16[1024,1024]{1,0:T(8,128)(2,1)}, bf16[1024,1024]{1,0:T(8,128)(2,1)}, u32[]{:S(2)}, u32[]{:S(2)}) collective-permute-start(bf16[1024,1024]{1,0:T(8,128)(2,1)} %select_bitcast_fusion), channel_id=1, source_target_pairs={{0,16},{1,17},{2,18},{3,19},{4,20},{5,21},{6,22},{7,23},{8,24},{9,... | collective-permute-start | bytes 6291464 | tf_op jit(solution)/shard_map/ppermute | solution.py:722
  33.3 30.7 %collective-permute-start.2 = (bf16[256,1024]{1,0:T(8,128)(2,1)}, bf16[256,1024]{1,0:T(8,128)(2,1)}, u32[]{:S(2)}, u32[]{:S(2)}) collective-permute-start(bf16[256,1024]{1,0:T(8,128)(2,1)} %fusion.27), channel_id=1, source_target_pairs={{0,16},{1,17},{2,18},{3,19},{4,20},{5,21},{6,22},{7,23},{8,24},{9,... | collective-permute-start | bytes 1572872 | tf_op jit(solution)/shard_map/ppermute | solution.py:722
  73.5 46.8 %collective-permute-start.12 = (bf16[1024,1024]{1,0:T(8,128)(2,1)}, bf16[1024,1024]{1,0:T(8,128)(2,1)}, u32[]{:S(2)}, u32[]{:S(2)}) collective-permute-start(bf16[1024,1024]{1,0:T(8,128)(2,1)} %get-tuple-element.55.refs_0_), channel_id=1, source_target_pairs={{0,2},{1,3},{2,0},{3,1},{4,6},{5,7},{6,4},{7,5},{8,10},{9,11},{10,... | collective-permute-start | bytes 6291464 | tf_op jit(solution)/shard_map/ppermute | solution.py:722
  78.4 135.5 %collective-permute-start.23 = (bf16[1040,768]{1,0:T(8,128)(2,1)}, bf16[1040,768]{1,0:T(8,128)(2,1)}, u32[]{:S(2)}, u32[]{:S(2)}) collective-permute-start(bf16[1040,768]{1,0:T(8,128)(2,1)} %copy.57), channel_id=1, source_target_pairs={{0,1},{2,3},{4,5},{6,7},{8,9},{10,11},{12,13},{14,15},{17,16},{19,... | collective-permute-start | bytes 4792328 | tf_op jit(solution)/shard_map/ppermute | solution.py:722
  81.2 78.1 %collective-permute-start.11 = (bf16[1024,1024]{1,0:T(8,128)(2,1)}, bf16[1024,1024]{1,0:T(8,128)(2,1)}, u32[]{:S(2)}, u32[]{:S(2)}) collective-permute-start(bf16[1024,1024]{1,0:T(8,128)(2,1)} %get-tuple-element.55.refs_0_), channel_id=1, source_target_pairs={{0,1},{1,0},{2,3},{3,2},{4,5},{5,4},{6,7},{7,6},{8,9},{9,8},{10,11... | collective-permute-start | bytes 6291464 | tf_op jit(solution)/shard_map/ppermute | solution.py:722
  81.3 134.2 %collective-permute-start.9 = (bf16[1024,1024]{1,0:T(8,128)(2,1)}, bf16[1024,1024]{1,0:T(8,128)(2,1)}, u32[]{:S(2)}, u32[]{:S(2)}) collective-permute-start(bf16[1024,1024]{1,0:T(8,128)(2,1)} %bitcast.70), channel_id=1, source_target_pairs={{0,16},{1,17},{2,18},{3,19},{4,20},{5,21},{6,22},{7,23},{8,24},{9,... | collective-permute-start | bytes 6291464 | tf_op jit(solution)/shard_map/ppermute | solution.py:722
  120.3 95.6 %collective-permute-start.26 = (bf16[1024,1024]{1,0:T(8,128)(2,1)}, bf16[1024,1024]{1,0:T(8,128)(2,1)}, u32[]{:S(2)}, u32[]{:S(2)}) collective-permute-start(bf16[1024,1024]{1,0:T(8,128)(2,1)} %get-tuple-element.18.refs_0_), channel_id=1, source_target_pairs={{0,1},{1,0},{2,3},{3,2},{4,5},{5,4},{6,7},{7,6},{8,9},{9,8},{10,11... | collective-permute-start | bytes 6291464 | tf_op jit(solution)/shard_map/ppermute | solution.py:722
  120.4 44.4 %collective-permute-start.7 = (bf16[512,256]{1,0:T(8,128)(2,1)S(1)}, bf16[512,256]{1,0:T(8,128)(2,1)S(1)}, u32[]{:S(2)}, u32[]{:S(2)}) collective-permute-start(bf16[512,256]{1,0:T(8,128)(2,1)S(1)} %pad_maximum_fusion.20), channel_id=1, source_target_pairs={{0,16},{1,17},{2,18},{3,19},{4,20},{5,21},{6,22},{7,23},{8,24},{9,... | collective-permute-start | bytes 786440 | tf_op jit(solution)/shard_map/ppermute | solution.py:722
  160.6 25.0 %collective-permute-start.13 = (bf16[512,1024]{1,0:T(8,128)(2,1)S(1)}, bf16[512,1024]{1,0:T(8,128)(2,1)S(1)}, u32[]{:S(2)}, u32[]{:S(2)}) collective-permute-start(bf16[512,1024]{1,0:T(8,128)(2,1)S(1)} %slice.339), channel_id=1, source_target_pairs={{0,2},{1,3},{2,0},{3,1},{4,6},{5,7},{6,4},{7,5},{8,10},{9,11},{10,... | collective-permute-start | bytes 3145736 | tf_op jit(solution)/shard_map/ppermute | solution.py:722
  164.9 46.3 %collective-permute-start.14 = (bf16[512,1024]{1,0:T(8,128)(2,1)S(1)}, bf16[512,1024]{1,0:T(8,128)(2,1)S(1)}, u32[]{:S(2)}, u32[]{:S(2)}) collective-permute-start(bf16[512,1024]{1,0:T(8,128)(2,1)S(1)} %slice.340), channel_id=1, source_target_pairs={{0,1},{1,0},{2,3},{3,2},{4,5},{5,4},{6,7},{7,6},{8,9},{9,8},{10,11... | collective-permute-start | bytes 3145736 | tf_op jit(solution)/shard_map/ppermute | solution.py:722
  185.5 29.9 %collective-permute-start.8 = (bf16[256,512]{1,0:T(8,128)(2,1)S(1)}, bf16[256,512]{1,0:T(8,128)(2,1)S(1)}, u32[]{:S(2)}, u32[]{:S(2)}) collective-permute-start(bf16[256,512]{1,0:T(8,128)(2,1)S(1)} %pad_maximum_fusion.22), channel_id=1, source_target_pairs={{0,2},{1,3},{2,0},{3,1},{4,6},{5,7},{6,4},{7,5},{8,10},{9,11},{10,... | collective-permute-start | bytes 786440 | tf_op jit(solution)/shard_map/ppermute | solution.py:722
  211.2 47.8 %collective-permute-start.27 = (bf16[1024,1024]{1,0:T(8,128)(2,1)}, bf16[1024,1024]{1,0:T(8,128)(2,1)}, u32[]{:S(2)}, u32[]{:S(2)}) collective-permute-start(bf16[1024,1024]{1,0:T(8,128)(2,1)} %get-tuple-element.18.refs_0_), channel_id=1, source_target_pairs={{0,2},{1,3},{2,0},{3,1},{4,6},{5,7},{6,4},{7,5},{8,10},{9,11},{10,... | collective-permute-start | bytes 6291464 | tf_op jit(solution)/shard_map/ppermute | solution.py:722
  213.9 49.3 %collective-permute-start.15 = (bf16[1024,1024]{1,0:T(8,128)(2,1)}, bf16[1024,1024]{1,0:T(8,128)(2,1)}, u32[]{:S(2)}, u32[]{:S(2)}) collective-permute-start(bf16[1024,1024]{1,0:T(8,128)(2,1)} %get-tuple-element.55.refs_0_), channel_id=1, source_target_pairs={{0,16},{1,17},{2,18},{3,19},{4,20},{5,21},{6,22},{7,23},{8,24},{9,... | collective-permute-start | bytes 6291464 | tf_op jit(solution)/shard_map/ppermute | solution.py:722
  215.4 49.2 %collective-permute-start.17 = (bf16[1024,1024]{1,0:T(8,128)(2,1)}, bf16[1024,1024]{1,0:T(8,128)(2,1)}, u32[]{:S(2)}, u32[]{:S(2)}) collective-permute-start(bf16[1024,1024]{1,0:T(8,128)(2,1)} %collective-permute-done.12.refs_2_), channel_id=1, source_target_pairs={{0,16},{1,17},{2,18},{3,19},{4,20},{5,21},{6,22},{7,23},{8,24},{9,... | collective-permute-start | bytes 6291464 | tf_op jit(solution)/shard_map/ppermute | solution.py:722
  215.5 49.1 %collective-permute-start.16 = (bf16[1024,1024]{1,0:T(8,128)(2,1)}, bf16[1024,1024]{1,0:T(8,128)(2,1)}, u32[]{:S(2)}, u32[]{:S(2)}) collective-permute-start(bf16[1024,1024]{1,0:T(8,128)(2,1)} %collective-permute-done.11.refs_1_), channel_id=1, source_target_pairs={{0,16},{1,17},{2,18},{3,19},{4,20},{5,21},{6,22},{7,23},{8,24},{9,... | collective-permute-start | bytes 6291464 | tf_op jit(solution)/shard_map/ppermute | solution.py:722
  215.9 48.7 %collective-permute-start.18 = (bf16[1024,1024]{1,0:T(8,128)(2,1)}, bf16[1024,1024]{1,0:T(8,128)(2,1)}, u32[]{:S(2)}, u32[]{:S(2)}) collective-permute-start(bf16[1024,1024]{1,0:T(8,128)(2,1)} %constant_dynamic-update-slice_fusion.refs_3_), channel_id=1, source_target_pairs={{0,16},{1,17},{2,18},{3,19},{4,20},{5,21},{6,22},{7,23},{8,24},{9,... | collective-permute-start | bytes 6291464 | tf_op jit(solution)/shard_map/ppermute | solution.py:722
  259.0 26.1 %collective-permute-start.28 = (bf16[512,1024]{1,0:T(8,128)(2,1)S(1)}, bf16[512,1024]{1,0:T(8,128)(2,1)}, u32[]{:S(2)}, u32[]{:S(2)}) collective-permute-start(bf16[512,1024]{1,0:T(8,128)(2,1)S(1)} %slice.354), channel_id=1, source_target_pairs={{0,2},{1,3},{2,0},{3,1},{4,6},{5,7},{6,4},{7,5},{8,10},{9,11},{10,... | collective-permute-start | bytes 3145736 | tf_op jit(solution)/shard_map/ppermute | solution.py:722
  263.2 34.2 %collective-permute-start.29 = (bf16[512,1024]{1,0:T(8,128)(2,1)}, bf16[512,1024]{1,0:T(8,128)(2,1)S(1)}, u32[]{:S(2)}, u32[]{:S(2)}) collective-permute-start(bf16[512,1024]{1,0:T(8,128)(2,1)} %slice.355), channel_id=1, source_target_pairs={{0,1},{1,0},{2,3},{3,2},{4,5},{5,4},{6,7},{7,6},{8,9},{9,8},{10,11... | collective-permute-start | bytes 3145736 | tf_op jit(solution)/shard_map/ppermute | solution.py:722
  278.4 48.7 %collective-permute-start.30 = (bf16[1024,1024]{1,0:T(8,128)(2,1)}, bf16[1024,1024]{1,0:T(8,128)(2,1)S(1)}, u32[]{:S(2)}, u32[]{:S(2)}) collective-permute-start(bf16[1024,1024]{1,0:T(8,128)(2,1)} %get-tuple-element.18.refs_0_), channel_id=1, source_target_pairs={{0,16},{1,17},{2,18},{3,19},{4,20},{5,21},{6,22},{7,23},{8,24},{9,... | collective-permute-start | bytes 6291464 | tf_op jit(solution)/shard_map/ppermute | solution.py:722
  285.1 42.1 %collective-permute-start.31 = (bf16[1024,1024]{1,0:T(8,128)(2,1)}, bf16[1024,1024]{1,0:T(8,128)(2,1)S(1)}, u32[]{:S(2)}, u32[]{:S(2)}) collective-permute-start(bf16[1024,1024]{1,0:T(8,128)(2,1)} %collective-permute-done.26.refs_1_), channel_id=1, source_target_pairs={{0,16},{1,17},{2,18},{3,19},{4,20},{5,21},{6,22},{7,23},{8,24},{9,... | collective-permute-start | bytes 6291464 | tf_op jit(solution)/shard_map/ppermute | solution.py:722
  297.4 29.8 %collective-permute-start.32 = (bf16[1024,1024]{1,0:T(8,128)(2,1)}, bf16[1024,1024]{1,0:T(8,128)(2,1)S(1)}, u32[]{:S(2)}, u32[]{:S(2)}) collective-permute-start(bf16[1024,1024]{1,0:T(8,128)(2,1)} %collective-permute-done.27.refs_2_), channel_id=1, source_target_pairs={{0,16},{1,17},{2,18},{3,19},{4,20},{5,21},{6,22},{7,23},{8,24},{9,... | collective-permute-start | bytes 6291464 | tf_op jit(solution)/shard_map/ppermute | solution.py:722
  298.1 29.1 %collective-permute-start.33 = (bf16[1024,1024]{1,0:T(8,128)(2,1)S(1)}, bf16[1024,1024]{1,0:T(8,128)(2,1)}, u32[]{:S(2)}, u32[]{:S(2)}) collective-permute-start(bf16[1024,1024]{1,0:T(8,128)(2,1)S(1)} %constant_dynamic-update-slice_fusion.2.refs_3_), channel_id=1, source_target_pairs={{0,16},{1,17},{2,18},{3,19},{4,20},{5,21},{6,22},{7,23},{8,24},{9,... | collective-permute-start | bytes 6291464 | tf_op jit(solution)/shard_map/ppermute | solution.py:722
  (89 other events, 708.1 us)
Sparse Core Ops, SparseCore 0:
  25.7 41.6 all-gather.2

commit v2 on v0

--- a/solution.py
+++ b/solution.py
@@ -1,6 +1,10 @@
+import functools
+
 import jax
 import jax.numpy as jnp
 from jax import lax
+from jax.experimental import pallas as pl
+from jax.experimental.pallas import tpu as pltpu
 from jax.sharding import PartitionSpec as P
 
 HEAD_DIM = 64
@@ -419,6 +423,789 @@
     )
 
 
+REACH = 512
+BF16 = jnp.bfloat16
+F32 = jnp.float32
+MESH = pl.DeviceIdType.MESH
+
+
+def dot_nn(a, b):
+    return lax.dot_general(a, b, (((1,), (0,)), ((), ())), preferred_element_type=F32)
+
+
+def dot_nt(a, b):
+    return lax.dot_general(a, b, (((1,), (1,)), ((), ())), preferred_element_type=F32)
+
+
+def dot_tn(a, b):
+    return lax.dot_general(a, b, (((0,), (0,)), ((), ())), preferred_element_type=F32)
+
+
+def norm_stats(rows):
+    middle = jnp.mean(rows, axis=-1, keepdims=True)
+    centred = rows - middle
+    inverse = lax.rsqrt(jnp.mean(centred * centred, axis=-1, keepdims=True) + EPSILON)
+    return centred * inverse, inverse
+
+
+def gelu_slope(pre):
+    square = pre * pre
+    bent = jnp.tanh(TANH_SCALE * (pre + CUBIC_TERM * square * pre))
+    return 0.5 * (1.0 + bent) + (0.5 * TANH_SCALE) * pre * (1.0 - bent * bent) * (
+        1.0 + (3.0 * CUBIC_TERM) * square
+    )
+
+
+def key_span(i, block):
+    return max(0, i - REACH // block) * block, (i + 1) * block
+
+
+def allowed_keys(i, block, seg_col_ref, seg_row_ref):
+    low, high = key_span(i, block)
+    seg_q = seg_col_ref[i * block : (i + 1) * block, :]
+    seg_k = seg_row_ref[:, low:high]
+    places_q = i * block + lax.broadcasted_iota(jnp.int32, (block, high - low), 0)
+    places_k = low + lax.broadcasted_iota(jnp.int32, (block, high - low), 1)
+    return (seg_q == seg_k) & (places_k <= places_q)
+
+
+def head_lanes(rows, h):
+    lane = lax.broadcasted_iota(jnp.int32, (rows, 128), 1)
+    return (lane < HEAD_DIM) if h == 0 else (lane >= HEAD_DIM)
+
+
+def both_halves(ref, *index):
+    return jnp.concatenate([ref[(*index, 0)], ref[(*index, 1)]], axis=1)
+
+
+class Wires:
+    def __init__(self, send, recv):
+        self.send, self.recv, self.count, self.sent = send, recv, 0, []
+
+    def copy(self, source, target, where):
+        k = self.count
+        self.count += 1
+        made = pltpu.make_async_remote_copy(
+            src_ref=source,
+            dst_ref=target,
+            send_sem=self.send.at[k],
+            recv_sem=self.recv.at[k],
+            device_id=where,
+            device_id_type=MESH,
+        )
+        self.sent.append(made)
+        return made
+
+    def forget(self, copy):
+        self.sent = [one for one in self.sent if one is not copy]
+
+
+WIRES = 40
+
+
+def step_kernel(
+    block,
+    model,
+    x_mine,
+    x_other,
+    cot_mine,
+    cot_other,
+    seg_col,
+    seg_row,
+    small,
+    wq,
+    up,
+    wo,
+    fc,
+    proj,
+    act,
+    grad,
+    down_sums,
+    up_sums,
+    xb,
+    cb,
+    sm,
+    wq_all,
+    up_all,
+    wo_all,
+    ff,
+    rows,
+    thin,
+    qkv,
+    o_out,
+    o_in,
+    middle,
+    norm2,
+    pre,
+    part_out,
+    part_in,
+    own_sum,
+    far_up,
+    grad_mid,
+    do_in,
+    dqkv,
+    dk_acc,
+    dv_acc,
+    c_out,
+    c_in,
+    y_out,
+    y_in,
+    wire_send,
+    wire_recv,
+    row_send,
+    row_recv,
+    wq_send,
+    wq_recv,
+    local_sem,
+    o_send,
+    o_recv,
+):
+    c = lax.axis_index("section")
+    t = lax.axis_index("tensor")
+    y, x = lax.div(t, 2), lax.rem(t, 2)
+    over_x, over_y = 2 * y + (1 - x), 2 * (1 - y) + x
+    mine, twin = 2 * y + c, 2 * y + (1 - c)
+    far, far_twin = 2 * (1 - y) + c, 2 * (1 - y) + (1 - c)
+    to_c, to_x, to_y = {"section": 1 - c}, {"tensor": over_x}, {"tensor": over_y}
+    to_xc = {"section": 1 - c, "tensor": over_x}
+    to_yc = {"section": 1 - c, "tensor": over_y}
+    here = c == x
+    wires = Wires(wire_send, wire_recv)
+    width = wq.shape[2]
+    factor = 8.0
+
+    barrier = pltpu.get_barrier_semaphore()
+    for peer in (to_c, to_x, to_y, to_xc, to_yc):
+        pl.semaphore_signal(barrier, inc=1, device_id=peer, device_id_type=MESH)
+    pl.semaphore_wait(barrier, 5)
+
+    def row_copy(source, target, k):
+        return pltpu.make_async_remote_copy(
+            src_ref=source,
+            dst_ref=target,
+            send_sem=row_send.at[k],
+            recv_sem=row_recv.at[k],
+            device_id=to_x,
+            device_id_type=MESH,
+        )
+
+    sm[c] = small[...]
+    small_copy = wires.copy(small, sm.at[c], to_c)
+    small_copy.start()
+    x_copy = row_copy(x_other, xb, 0)
+
+    @pl.when(here)
+    def _():
+        x_copy.start()
+        xb[...] = x_mine[...]
+
+    def wq_pair(k, where):
+        return [
+            pltpu.make_async_remote_copy(
+                src_ref=source,
+                dst_ref=target.at[c],
+                send_sem=wq_send.at[k, j],
+                recv_sem=wq_recv.at[c, j],
+                device_id=where,
+                device_id_type=MESH,
+            )
+            for j, (source, target) in enumerate(((wq, wq_all), (up, up_all)))
+        ]
+
+    def wq_local(layer):
+        return [
+            pltpu.make_async_copy(source, target.at[layer], wq_recv.at[layer, j])
+            for j, (source, target) in enumerate(((wq, wq_all), (up, up_all)))
+        ]
+
+    def send_wq():
+        for copy in wq_pair(1, {"section": x, "tensor": over_x}):
+            copy.start()
+
+        @pl.when(here)
+        def _():
+            for copy in wq_local(c):
+                copy.start()
+
+        @pl.when(jnp.logical_not(here))
+        def _():
+            for copy in wq_pair(0, to_c):
+                copy.start()
+
+    def sent_wq():
+        for copy in wq_pair(1, to_x):
+            copy.wait_send()
+
+        @pl.when(jnp.logical_not(here))
+        def _():
+            for copy in wq_pair(0, to_c):
+                copy.wait_send()
+
+    pl.when(c == 0)(send_wq)
+
+    locals_ = [
+        pltpu.make_async_copy(source, target, local_sem.at[k])
+        for k, (source, target) in enumerate(
+            ((fc, ff.at[c, 0, 0]), (proj, ff.at[c, 1, 0]), (wo, wo_all.at[c, t]))
+        )
+    ]
+    for copy in locals_:
+        copy.start()
+    ff_twin = [wires.copy(one, ff.at[c, k, 0], to_c) for k, one in enumerate((fc, proj))]
+    ff_y = [wires.copy(one, ff.at[c, k, 1], to_y) for k, one in enumerate((fc, proj))]
+    ff_y_twin = [wires.copy(ff.at[c, k, 1], ff.at[c, k, 1], to_c) for k in range(2)]
+    wo_twin = wires.copy(wo, wo_all.at[c, t], to_c)
+    wo_x = wires.copy(wo, wo_all.at[c, t], to_x)
+    wo_y = wires.copy(wo, wo_all.at[c, t], to_y)
+    half = width // 2
+    wo_dy = wires.copy(
+        wo_all.at[c, over_x, pl.ds(0, half)], wo_all.at[c, over_x, pl.ds(0, half)], to_y
+    )
+    wo_dx = wires.copy(
+        wo_all.at[c, over_y, pl.ds(half, half)], wo_all.at[c, over_y, pl.ds(half, half)], to_x
+    )
+    corner = 2 * (1 - y) + (1 - x)
+    wo_twins = [
+        wires.copy(wo_all.at[c, q], wo_all.at[c, q], to_c) for q in (over_x, over_y, corner)
+    ]
+
+    def start_ff(layer):
+        @pl.when(c == layer)
+        def _():
+            for copy in ff_y:
+                copy.start()
+
+    def pass_ff(layer):
+        @pl.when(c == layer)
+        def _():
+            for copy, onward in zip(ff_y, ff_y_twin):
+                copy.wait_recv()
+                onward.start()
+
+        @pl.when(c != layer)
+        def _():
+            for onward in ff_y_twin:
+                onward.wait_recv()
+
+    start_ff(0)
+    for copy in ff_twin + [wo_twin]:
+        copy.start()
+
+    def arrived_wq(layer):
+        for copy in wq_local(layer):
+            copy.wait()
+
+    def qkv_block(layer, b):
+        normed = rows[layer, b]
+        down = sm[layer, 16:32, :].astype(BF16)
+        low = dot_nt(normed, down)
+        low_b = low.astype(BF16)
+        thin[layer, b] = low_b
+        at = pl.ds(pl.multiple_of(b * block, block), block)
+        for k in range(3):
+            made = dot_nn(normed, wq_all[layer, k])
+            if k == 0:
+                made = made + factor * dot_nn(low_b, up_all[layer, 0])
+            if k == 2:
+                made = made + factor * dot_nn(low_b, up_all[layer, 1])
+            made = made.astype(BF16)
+            qkv[layer, k, 0, at, :] = made[:, :128]
+            qkv[layer, k, 1, at, :] = made[:, 128:]
+
+    def attend(layer, i):
+        low, high = key_span(i, block)
+        at = slice(i * block, (i + 1) * block)
+        allowed = allowed_keys(i, block, seg_col, seg_row)
+
+        def one_pair(pair, carry):
+            queries = qkv[layer, 0, pair, at, :] * BF16(HEAD_DIM**-0.5)
+            keys = qkv[layer, 1, pair, low:high, :]
+            values = qkv[layer, 2, pair, low:high, :]
+            parts = []
+            for h in range(2):
+                picked = jnp.where(head_lanes(block, h), queries, BF16(0))
+                scores = jnp.where(allowed, dot_nt(picked, keys), MASKED)
+                exponent = jnp.exp(scores - jnp.max(scores, axis=-1, keepdims=True))
+                total = jnp.sum(exponent, axis=-1, keepdims=True)
+                parts.append(dot_nn(exponent.astype(BF16), values) / total)
+            o_out[i, pair] = jnp.where(head_lanes(block, 0), parts[0], parts[1]).astype(BF16)
+            return carry
+
+        lax.fori_loop(0, 2, one_pair, 0)
+
+    def exchange_piece(i, target, phase):
+        return pltpu.make_async_remote_copy(
+            src_ref=o_out.at[i],
+            dst_ref=target.at[mine],
+            send_sem=o_send.at[i],
+            recv_sem=o_recv.at[phase, mine],
+            device_id={"section": i % 2, "tensor": 2 * (i // 2) + x},
+            device_id_type=MESH,
+        )
+
+    def send_piece(i, target, phase):
+        @pl.when(mine == i)
+        def _():
+            target[mine] = o_out[i]
+
+        @pl.when(mine != i)
+        def _():
+            exchange_piece(i, target, phase).start()
+
+    def wait_pieces(target, phase):
+        for i in range(4):
+
+            @pl.when(mine != i)
+            def _():
+                exchange_piece(i, target, phase).wait_send()
+                pltpu.make_async_copy(o_out.at[i], target.at[i], o_recv.at[phase, i]).wait()
+
+    def hidden_half(layer, who, source, q):
+        total = None
+        for cut in range(2):
+            lanes = slice(cut * model // 2, (cut + 1) * model // 2)
+            made = dot_nn(source, ff[layer, 0, q, :, lanes])
+            pre[layer, who, q, :, lanes] = made.astype(BF16)
+            term = dot_nn(gelu_tanh(made).astype(BF16), ff[layer, 1, q, lanes, :])
+            total = term if total is None else total + term
+        return total
+
+    def hidden_back(layer, who, upstream, q):
+        total = None
+        for cut in range(2):
+            lanes = slice(cut * model // 2, (cut + 1) * model // 2)
+            grad_hidden = dot_nt(upstream, ff[layer, 1, q, lanes, :])
+            slope = gelu_slope(pre[layer, who, q, :, lanes].astype(F32))
+            term = dot_nt((grad_hidden * slope).astype(BF16), ff[layer, 0, q, :, lanes])
+            total = term if total is None else total + term
+        return total
+
+    @pl.when(jnp.logical_not(here))
+    def _():
+        x_copy.wait_recv()
+
+    small_copy.wait_recv()
+
+    for layer in range(2):
+        source = xb if layer == 0 else act.at[0]
+        unit, _ = norm_stats(source[...].astype(F32))
+        rows[layer, mine] = (unit * sm[layer, 0:1, :]).astype(BF16)
+        row_y = wires.copy(rows.at[layer, mine], rows.at[layer, mine], to_y)
+        row_c = wires.copy(rows.at[layer, mine], rows.at[layer, mine], to_c)
+        row_yc = wires.copy(rows.at[layer, far], rows.at[layer, far], to_c)
+        row_y.start()
+        row_c.start()
+        arrived_wq(layer)
+        if layer == 0:
+            for copy in (wo_x, wo_y):
+                copy.start()
+        qkv_block(layer, mine)
+        row_c.wait_recv()
+        qkv_block(layer, twin)
+        row_y.wait_recv()
+        row_yc.start()
+        qkv_block(layer, far)
+        row_yc.wait_recv()
+        qkv_block(layer, far_twin)
+        for i in range(4):
+            attend(layer, i)
+            send_piece(i, o_in, layer)
+        if layer == 0:
+            locals_[2].wait()
+            wo_x.wait_recv()
+            wo_dy.start()
+            wo_twins[0].start()
+            wo_y.wait_recv()
+            wo_dx.start()
+            wo_twins[1].start()
+            wo_dy.wait_recv()
+            wo_dx.wait_recv()
+            wo_twins[2].start()
+            wo_twin.wait_recv()
+            for copy in wo_twins:
+                copy.wait_recv()
+        wait_pieces(o_in, layer)
+        stream = source[...].astype(F32)
+        for q in range(4):
+            stream = stream + dot_nn(both_halves(o_in, q), wo_all[layer, q])
+        middle[layer] = stream
+        unit, _ = norm_stats(stream)
+        norm2[0] = (unit * sm[layer, 8:9, :]).astype(BF16)
+        norm_x = wires.copy(norm2.at[0], norm2.at[1], to_x)
+        norm_x.start()
+        if layer == 0:
+            for copy in locals_[:2]:
+                copy.wait()
+            for copy in ff_twin:
+                copy.wait_recv()
+        own_sum[...] = hidden_half(layer, 0, norm2[0], 0)
+        norm_x.wait_recv()
+        away = hidden_half(layer, 1, norm2[1], 0)
+        pass_ff(layer)
+        away = away + hidden_half(layer, 1, norm2[1], 1)
+        part_out[...] = away.astype(BF16)
+        part_x = wires.copy(part_out, part_in.at[0], to_x)
+        part_x.start()
+        if layer == 0:
+            start_ff(1)
+            pl.when(c == 1)(send_wq)
+        stream = middle[layer] + own_sum[...] + hidden_half(layer, 0, norm2[0], 1)
+        part_x.wait()
+        wires.forget(part_x)
+        norm_x.wait_send()
+        wires.forget(norm_x)
+        act[layer] = (stream + part_in[0].astype(F32)).astype(BF16)
+        if layer == 0:
+            cot_copies = [row_copy(cot_other, cb.at[0], 1), row_copy(cot_mine, cb.at[1], 2)]
+
+            @pl.when(here)
+            def _():
+                for copy in cot_copies:
+                    copy.start()
+                cb[0] = cot_mine[...]
+                cb[1] = cot_other[...]
+
+    @pl.when(jnp.logical_not(here))
+    def _():
+        for copy in cot_copies:
+            copy.wait_recv()
+
+    for layer in (1, 0):
+        upstream = cb[0] if layer == 1 else grad[1]
+        if layer == 1:
+            away = hidden_back(layer, 1, cb[1], 0) + hidden_back(layer, 1, cb[1], 1)
+        else:
+            up_x = wires.copy(grad.at[1], far_up, to_x)
+            up_x.start()
+            own_sum[...] = hidden_back(layer, 0, upstream, 0) + hidden_back(layer, 0, upstream, 1)
+            up_x.wait_recv()
+            away = hidden_back(layer, 1, far_up[...], 0) + hidden_back(layer, 1, far_up[...], 1)
+        part_out[...] = away.astype(BF16)
+        part_x = wires.copy(part_out, part_in.at[1], to_x)
+        part_x.start()
+        if layer == 1:
+            own_sum[...] = hidden_back(layer, 0, upstream, 0) + hidden_back(layer, 0, upstream, 1)
+        unit, inverse = norm_stats(middle[layer])
+        part_x.wait()
+        wires.forget(part_x)
+        grad_norm = own_sum[...] + part_in[1].astype(F32)
+        grad_middle = upstream.astype(F32) + normalize_back(
+            grad_norm, unit, inverse, sm[layer, 8:9, :]
+        )
+        grad_mid[...] = grad_middle
+        grad_b = grad_middle.astype(BF16)
+        for q in range(4):
+            made = dot_nt(grad_b, wo_all[layer, q]).astype(BF16)
+            o_out[q, 0] = made[:, :128]
+            o_out[q, 1] = made[:, 128:]
+            send_piece(q, do_in, 2 + layer)
+        wait_pieces(do_in, 2 + layer)
+
+        def back_pair(pair, carry):
+            dk_acc[...] = jnp.zeros_like(dk_acc)
+            dv_acc[...] = jnp.zeros_like(dv_acc)
+            for i in range(4):
+                low, high = key_span(i, block)
+                at = slice(i * block, (i + 1) * block)
+                allowed = allowed_keys(i, block, seg_col, seg_row)
+                queries = qkv[layer, 0, pair, at, :] * BF16(HEAD_DIM**-0.5)
+                keys = qkv[layer, 1, pair, low:high, :]
+                values = qkv[layer, 2, pair, low:high, :]
+                grads = do_in[i, pair]
+                parts = []
+                for h in range(2):
+                    lanes = head_lanes(block, h)
+                    picked = jnp.where(lanes, queries, BF16(0))
+                    given = jnp.where(lanes, grads, BF16(0))
+                    scores = jnp.where(allowed, dot_nt(picked, keys), MASKED)
+                    exponent = jnp.exp(scores - jnp.max(scores, axis=-1, keepdims=True))
+                    soft = exponent * (1.0 / jnp.sum(exponent, axis=-1, keepdims=True))
+                    weighted = soft * dot_nt(given, values)
+                    grad_scores = (
+                        weighted - soft * jnp.sum(weighted, axis=-1, keepdims=True)
+                    ).astype(BF16)
+                    parts.append(dot_nn(grad_scores, keys))
+                    dk_acc[low:high, :] += dot_tn(grad_scores, picked)
+                    dv_acc[low:high, :] += dot_tn(soft.astype(BF16), given)
+                dqkv[0, pair, at, :] = (
+                    jnp.where(head_lanes(block, 0), parts[0], parts[1]) * HEAD_DIM**-0.5
+                ).astype(BF16)
+            dqkv[1, pair] = dk_acc[...].astype(BF16)
+            dqkv[2, pair] = dv_acc[...].astype(BF16)
+            return carry
+
+        lax.fori_loop(0, 2, back_pair, 0)
+        down = sm[layer, 16:32, :].astype(BF16)
+
+        def block_grad(b, first):
+            at = pl.ds(pl.multiple_of(b * block, block), block)
+            parts = [
+                jnp.concatenate([dqkv[k, 0, at, :], dqkv[k, 1, at, :]], axis=1) for k in range(3)
+            ]
+            low = factor * (
+                dot_nt(parts[0], up_all[layer, 0]) + dot_nt(parts[2], up_all[layer, 1])
+            )
+            low_b = low.astype(BF16)
+            term = dot_nn(low_b, down)
+            for k in range(3):
+                term = term + dot_nt(parts[k], wq_all[layer, k])
+            kept = thin[layer, b]
+            to_down = dot_tn(low_b, rows[layer, b])
+            to_up = [factor * dot_tn(kept, parts[0]), factor * dot_tn(kept, parts[2])]
+            if first:
+                down_sums[layer] = to_down
+                up_sums[layer, 0], up_sums[layer, 1] = to_up
+            else:
+                down_sums[layer] += to_down
+                up_sums[layer, 0] += to_up[0]
+                up_sums[layer, 1] += to_up[1]
+            return term
+
+        c_far = wires.copy(c_out.at[0], c_in.at[0], to_c)
+        c_near = wires.copy(c_out.at[1], c_in.at[1], to_c)
+        y_far = wires.copy(y_out, y_in, to_y)
+        c_out[0] = block_grad(far_twin, True).astype(BF16)
+        c_far.start()
+        term = block_grad(far, False)
+        c_far.wait_recv()
+        y_out[...] = (term + c_in[0].astype(F32)).astype(BF16)
+        y_far.start()
+        c_out[1] = block_grad(twin, False).astype(BF16)
+        c_near.start()
+        term = block_grad(mine, False)
+        c_near.wait_recv()
+        term = term + c_in[1].astype(F32)
+        source = xb if layer == 0 else act.at[0]
+        unit, inverse = norm_stats(source[...].astype(F32))
+        y_far.wait_recv()
+        grad_norm = term + y_in[...].astype(F32)
+        grad[layer] = (
+            grad_mid[...] + normalize_back(grad_norm, unit, inverse, sm[layer, 0:1, :])
+        ).astype(BF16)
+        for copy in (c_far, c_near, y_far):
+            copy.wait_send()
+            wires.forget(copy)
+
+    @pl.when(here)
+    def _():
+        x_copy.wait_send()
+        for copy in cot_copies:
+            copy.wait_send()
+
+    sent_wq()
+    for copy in wires.sent:
+        copy.wait_send()
+
+
+def step_call(block, model, width, rank, operands):
+    slots = 4 * block
+    in_vmem = pl.BlockSpec(memory_space=pltpu.VMEM)
+    in_hbm = pl.BlockSpec(memory_space=pl.ANY)
+    return pl.pallas_call(
+        functools.partial(step_kernel, block, model),
+        out_shape=(
+            jax.ShapeDtypeStruct((2, block, model), BF16),
+            jax.ShapeDtypeStruct((2, block, model), BF16),
+            jax.ShapeDtypeStruct((2, 16, model), F32),
+            jax.ShapeDtypeStruct((2, 2, 16, width), F32),
+        ),
+        in_specs=[in_vmem] * 7 + [in_hbm] * 5,
+        out_specs=[in_vmem] * 4,
+        scratch_shapes=[
+            pltpu.VMEM((block, model), BF16),
+            pltpu.VMEM((2, block, model), BF16),
+            pltpu.VMEM((2, 32, model), F32),
+            pltpu.VMEM((2, 3, model, width), BF16),
+            pltpu.VMEM((2, 2, 16, width), BF16),
+            pltpu.VMEM((2, 4, width, model), BF16),
+            pltpu.VMEM((2, 2, 2, model, model), BF16),
+            pltpu.VMEM((2, 4, block, model), BF16),
+            pltpu.VMEM((2, 4, block, 16), BF16),
+            pltpu.VMEM((2, 3, 2, slots, 128), BF16),
+            pltpu.VMEM((4, 2, block, 128), BF16),
+            pltpu.VMEM((4, 2, block, 128), BF16),
+            pltpu.VMEM((2, block, model), F32),
+            pltpu.VMEM((2, block, model), BF16),
+            pltpu.VMEM((2, 2, 2, block, model), BF16),
+            pltpu.VMEM((block, model), BF16),
+            pltpu.VMEM((2, block, model), BF16),
+            pltpu.VMEM((block, model), F32),
+            pltpu.VMEM((block, model), BF16),
+            pltpu.VMEM((block, model), F32),
+            pltpu.VMEM((4, 2, block, 128), BF16),
+            pltpu.VMEM((3, 2, slots, 128), BF16),
+            pltpu.VMEM((slots, 128), F32),
+            pltpu.VMEM((slots, 128), F32),
+            pltpu.VMEM((2, block, model), BF16),
+            pltpu.VMEM((2, block, model), BF16),
+            pltpu.VMEM((block, model), BF16),
+            pltpu.VMEM((block, model), BF16),
+            pltpu.SemaphoreType.DMA((WIRES,)),
+            pltpu.SemaphoreType.DMA((WIRES,)),
+            pltpu.SemaphoreType.DMA((3,)),
+            pltpu.SemaphoreType.DMA((3,)),
+            pltpu.SemaphoreType.DMA((2, 2)),
+            pltpu.SemaphoreType.DMA((2, 2)),
+            pltpu.SemaphoreType.DMA((3,)),
+            pltpu.SemaphoreType.DMA((4,)),
+            pltpu.SemaphoreType.DMA((4, 4)),
+        ],
+        compiler_params=pltpu.CompilerParams(
+            collective_id=0, has_side_effects=True, vmem_limit_bytes=61 * 1024 * 1024
+        ),
+    )(*operands)
+
+
+ROUTE_AXES = ("section", "dp", "tensor")
+
+
+def route(planes, rule):
+    pairs = []
+    for c in range(2):
+        for z in range(planes):
+            for y in range(2):
+                for x in range(2):
+                    target = rule(c, z, y, x)
+                    if target is not None:
+                        tc, tz, ty, tx = target
+                        pairs.append(
+                            ((c * planes + z) * 4 + 2 * y + x, (tc * planes + tz) * 4 + 2 * ty + tx)
+                        )
+    return pairs
+
+
+def fast_body(
+    planes,
+    inputs,
+    segments,
+    cotangent,
+    gain_attn,
+    joint_projection_weight,
+    query_down_factor,
+    query_up_factor,
+    value_down_factor,
+    value_up_factor,
+    w_out,
+    gain_mlp,
+    w_fc,
+    w_proj,
+):
+    core = lax.axis_index("section")
+    place = lax.axis_index("tensor")
+    y, x = place // 2, place % 2
+    block, _, model = inputs.shape
+    width = joint_projection_weight.shape[3]
+    rank = query_down_factor.shape[2]
+    core_0, x_0 = core == 0, x == 0
+
+    def sent(value, rule):
+        return lax.ppermute(value, ROUTE_AXES, route(planes, rule))
+
+    def both_rows(array):
+        return (
+            jnp.where(x_0, array[:, 0], array[:, 1]),
+            jnp.where(x_0, array[:, 1], array[:, 0]),
+        )
+
+    segment_row = jnp.where(x_0, segments[0], segments[1])
+    blank = jnp.zeros((7, model), F32)
+    small = jnp.concatenate(
+        [
+            gain_attn,
+            blank,
+            gain_mlp,
+            blank,
+            query_down_factor[0].T.astype(F32),
+            value_down_factor[0].T.astype(F32),
+            jnp.zeros((16 - 2 * rank, model), F32),
+        ],
+        axis=0,
+    )
+    ups = jnp.stack(
+        [
+            jnp.pad(query_up_factor[0], ((0, 16 - rank), (0, 0))),
+            jnp.pad(value_up_factor[0], ((rank, 16 - 2 * rank), (0, 0))),
+        ]
+    )
+    acts, grads, down_sums, up_sums = step_call(
+        block,
+        model,
+        width,
+        rank,
+        (
+            *both_rows(inputs),
+            *both_rows(cotangent),
+            segment_row[:, None],
+            segment_row[None, :],
+            small,
+            jnp.swapaxes(joint_projection_weight[0], 0, 1),
+            ups,
+            w_out[0],
+            w_fc[0],
+            w_proj[0],
+        ),
+    )
+    totals = []
+    for layer in (1, 0):
+        placed_up = [
+            lax.dynamic_update_slice_in_dim(
+                jnp.zeros((rank, model), F32),
+                up_sums[layer, k, k * rank : (k + 1) * rank],
+                (2 * y + core) * width,
+                1,
+            )
+            for k in range(2)
+        ]
+        total = jnp.concatenate([down_sums[layer, : 2 * rank], *placed_up], axis=0)
+        total = total + sent(total, lambda c, z, y, x: (1 - c, z, y, x))
+        total = total + sent(total, lambda c, z, y, x: (c, z, y, 1 - x))
+        total = total + sent(total, lambda c, z, y, x: (c, z, 1 - y, x))
+        bit = 1
+        while bit < planes:
+            total = total + sent(total, lambda c, z, y, x: (c, z ^ bit, y, x))
+            bit *= 2
+        totals.append(total)
+
+    def placed(pair):
+        same, other = [], []
+        for layer in range(2):
+            same.append(
+                sent(pair[layer], lambda c, z, y, x: (layer, z, y, x) if c == x else None)
+            )
+            other.append(
+                sent(pair[layer], lambda c, z, y, x: (layer, z, y, 1 - x) if c != x else None)
+            )
+        same = jnp.where(core_0, same[0], same[1])
+        other = jnp.where(core_0, other[0], other[1])
+        return jnp.stack([jnp.where(x_0, same, other), jnp.where(x_0, other, same)], axis=1)[None]
+
+    total = jnp.where(core_0, totals[1], totals[0])
+    return (
+        placed(acts),
+        placed(grads),
+        total[:rank].T[None],
+        total[2 * rank : 3 * rank][None],
+        total[rank : 2 * rank].T[None],
+        total[3 * rank :][None],
+    )
+
+
+def fits_fast(mesh, shapes):
+    planes = mesh.shape["dp"]
+    slots, rows_all, model = shapes[0]
+    return (
+        mesh.shape["section"] == 2
+        and mesh.shape["tensor"] == 4
+        and planes & (planes - 1) == 0
+        and rows_all == 2 * planes
+        and slots == 1024
+        and model == 1024
+        and shapes[4][3] == 1024
+        and shapes[5][2] == 4
+        and shapes[11][2] == 4096
+    )
+
+
 def solution(mesh):
     placed = (
         P("tensor", "dp", None),
@@ -435,17 +1222,26 @@
         P("section", None, "tensor"),
         P("section", "tensor", None),
     )
-    return jax.shard_map(
-        body,
-        mesh=mesh,
-        in_specs=placed,
-        out_specs=(
-            P("section", "tensor", "dp", None),
-            P("section", "tensor", "dp", None),
-            P("section", None, None),
-            P("section", None, None),
-            P("section", None, None),
-            P("section", None, None),
-        ),
-        check_vma=False,
-    )
+
+    def mapped(picked):
+        return jax.shard_map(
+            picked,
+            mesh=mesh,
+            in_specs=placed,
+            out_specs=(
+                P("section", "tensor", "dp", None),
+                P("section", "tensor", "dp", None),
+                P("section", None, None),
+                P("section", None, None),
+                P("section", None, None),
+                P("section", None, None),
+            ),
+            check_vma=False,
+        )
+
+    def choose(*args):
+        if fits_fast(mesh, [a.shape for a in args]):
+            return mapped(functools.partial(fast_body, mesh.shape["dp"]))(*args)
+        return mapped(body)(*args)
+
+    return choose

time: 1900 us -> 419 us (0.22)
  waiting for transfers between devices: 1140 us -> 22.9 us
  matrix products: 444 us -> 0 us
  Pallas kernels: 0 us -> 332 us
  other arithmetic: 145 us -> 8.49 us
  local copies, waits for them, and re-layouts: 113 us -> 19.6 us
    all_gather x18 -> x0, waiting for transfers between devices: 558 us -> none  [the longest x6 179 us: mlp_pre(): lax.all_gather(normed_b, 'tensor', axis=0, tiled=True)]
    reduce_scatter x15 -> x0, waiting for transfers between devices: 467 us -> none  [the longest x6 179 us: attention_project(): lax.psum_scatter(jnp.einsum('srf,fd->srd', attended_b, w_out, preferred_e...]
    dot_general x123 -> x0, matrix products: 398 us -> none  [the longest x12 56.8 us: one_block(): jnp.einsum('rhqk,krhe->qrhe', weights_soft, values_all, preferred_element...]
    pallas_call x0 -> x1, Pallas kernels: none -> 332 us  [step_call(): pl.pallas_call(functools.partial(step_kernel, block, model), out_shape=(j...]
    psum x1 -> x0, waiting for transfers between devices: 105 us -> none  [body(): lax.psum((gradient_totals[0], full_query, gradient_totals[2], full_value)...]
    sub x6 -> x0, matrix products: 45.3 us -> none  [one_block(): exponent = jnp.exp(scores - row_max)]
    convert_element_type x18 -> x2, other arithmetic: 46.5 us -> 1.4 us  [the longest x1 0.7 us: fast_body(): value_down_factor[0].T.astype(F32)]
    another operation x29 -> x6, local copies, waits for them, and re-layouts: 45.4 us -> 1.39 us  [the longest x2 1.37 us: fast_body(): jnp.stack([jnp.pad(query_up_factor[0], ((0, 16 - rank), (0, 0))), jnp.pad...]
  transfers between devices with their start and end apart: 38 -> 18, of which waited for: 37 -> 6; matrix products, arithmetic and copies ran while one was open for 7% -> 1% of each run, Pallas kernels for 0% -> 0%
where the time goes in v2:
time: 419 us; the launch traced here: 411 us
  Pallas kernels  332 us (79%)
  starting transfers between devices  27.2 us (6%)
  waiting for transfers between devices  22.9 us (5%)
  local copies, waits for them, and re-layouts  19.6 us (5%)
  other arithmetic  8.49 us (2%)
    pallas_call x1, Pallas kernels, step_call(): pl.pallas_call(functools.partial(step_kernel, block, model), out_shape=(j...  332 us
    ppermute x18, starting transfers between devices, sent(): return lax.ppermute(value, ROUTE_AXES, route(planes, rule))  27.2 us
    ppermute x18, waiting for transfers between devices, sent(): return lax.ppermute(value, ROUTE_AXES, route(planes, rule))  22.9 us
  transfers between devices with their start and end apart: 18, of which 6 were waited for; matrix products, arithmetic and copies ran while one was open for 1% of the time, Pallas kernels for 0%

profile of v2, /device:TPU:0, one launch (start us, length us, event | category | flops | bytes accessed | tf_op | source)
XLA Modules:
  0.0 411.2 jit_solution(11864479998450668784)
XLA Ops:
  1.4 1.4 broadcast_select_fusion.4.seg_row
  6.6 3.4 fusion.3
  10.0 1.5 fusion.2
  13.4 1.3 select_bitcast_fusion.4
  14.7 2.5 concatenate.9.small
  17.2 331.7 %shard_map.172 = (bf16[2,256,1024]{2,1,0:T(8,128)(2,1)}, bf16[2,256,1024]{2,1,0:T(8,128)(2,1)}, f32[2,16,1024]{2,1,0:T(8,128)}, f32[2,2,16,256]{3,2,1,0:T(8,128)}) custom-call(bf16[256,1024]{1,0:T(8,128)(2,1)} %get-tuple-element.33.x_mine, bf16[256,1024]{1,0:T(8,128)(2,1)} %get-tuple-element.32.x_other, bf16[256,1024]{1,0:T(8,128)(2,1)} %get-tuple-element.31.cot_mine, ...), custom_call_target="tpu_custom_call" | custom-call | tf_op jit(solution)/shard_map/pallas_call | solution.py:1004
  348.9 1.4 slice_bitcast_fusion.2
  350.3 1.5 collective-permute-start.3
  351.8 2.2 collective-permute-start.1
  358.8 2.7 collective-permute-start.14
  361.6 9.0 %collective-permute-done.14 = f32[16,1024]{1,0:T(8,128)S(1)} collective-permute-done((f32[16,1024]{1,0:T(8,128)S(1)}, f32[16,1024]{1,0:T(8,128)S(1)}, u32[]{:S(2)}, u32[]{:S(2)}) %collective-permute-start.14) | collective-permute-done | bytes 65568 | tf_op jit(solution)/shard_map/ppermute | solution.py:1102
  372.9 2.2 collective-permute-done.15
  375.0 1.6 collective-permute-start.16
  377.5 2.6 collective-permute-done.16
  380.1 2.1 collective-permute-start.17
  382.2 2.0 collective-permute-start.12
  384.3 1.7 collective-permute-done.17
  388.1 5.8 %collective-permute-start.5 = (bf16[256,1024]{1,0:T(8,128)(2,1)S(1)}, bf16[256,1024]{1,0:T(8,128)(2,1)}, u32[]{:S(2)}, u32[]{:S(2)}) collective-permute-start(bf16[256,1024]{1,0:T(8,128)(2,1)S(1)} %get-tuple-element.34), channel_id=1, source_target_pairs={{0,16},{2,18},{4,20},{6,22},{8,24},{10,26},{12,28},{14,30},{17,17}... | collective-permute-start | bytes 1572872 | tf_op jit(solution)/shard_map/ppermute | solution.py:1102
  394.0 1.5 collective-permute-start.6
  396.3 1.4 collective-permute-start.4
  398.4 6.6 %collective-permute-done.6 = bf16[256,1024]{1,0:T(8,128)(2,1)S(1)} collective-permute-done((bf16[256,1024]{1,0:T(8,128)(2,1)S(1)}, bf16[256,1024]{1,0:T(8,128)(2,1)S(1)}, u32[]{:S(2)}, u32[]{:S(2)}) %collective-permute-start.6) | collective-permute-done | bytes 524320 | tf_op jit(solution)/shard_map/ppermute | solution.py:1102
  405.0 1.4 select_bitcast_fusion.1
  406.6 2.0 copy.31
  408.7 2.0 copy.30
  (68 shorter events, 18.3 us)
Async XLA Ops:
  6.6 3.4 copy-start
  13.4 1.3 copy-start.4
  13.4 1.3 copy-start.5
  348.9 6.5 %copy-start.3 = (f32[2,16,1024]{2,1,0:T(8,128)S(1)}, f32[2,16,1024]{2,1,0:T(8,128)}, u32[]{:S(2)}) copy-start(f32[2,16,1024]{2,1,0:T(8,128)} %get-tuple-element.12) | copy-start | bytes 393220
  348.9 35.3 %copy-start.1 = (bf16[2,256,1024]{2,1,0:T(8,128)(2,1)S(1)}, bf16[2,256,1024]{2,1,0:T(8,128)(2,1)}, u32[]{:S(2)}) copy-start(bf16[2,256,1024]{2,1,0:T(8,128)(2,1)} %get-tuple-element.11) | copy-start | bytes 3145732
  350.3 37.8 %collective-permute-start.3 = (bf16[256,1024]{1,0:T(8,128)(2,1)S(1)}, bf16[256,1024]{1,0:T(8,128)(2,1)}, u32[]{:S(2)}, u32[]{:S(2)}) collective-permute-start(bf16[256,1024]{1,0:T(8,128)(2,1)S(1)} %get-tuple-element.36), channel_id=1, source_target_pairs={{1,16},{3,18},{5,20},{7,22},{9,24},{11,26},{13,28},{15,30},{16,17}... | collective-permute-start | bytes 1572872 | tf_op jit(solution)/shard_map/ppermute | solution.py:1102
  351.8 42.2 %collective-permute-start.1 = (bf16[256,1024]{1,0:T(8,128)(2,1)S(1)}, bf16[256,1024]{1,0:T(8,128)(2,1)}, u32[]{:S(2)}, u32[]{:S(2)}) collective-permute-start(bf16[256,1024]{1,0:T(8,128)(2,1)S(1)} %get-tuple-element.36), channel_id=1, source_target_pairs={{0,16},{2,18},{4,20},{6,22},{8,24},{10,26},{12,28},{14,30},{17,17}... | collective-permute-start | bytes 1572872 | tf_op jit(solution)/shard_map/ppermute | solution.py:1102
  355.4 3.4 collective-permute-start.13
  357.0 4.6 %collective-permute-start.8 = (f32[16,1024]{1,0:T(8,128)S(1)}, f32[16,1024]{1,0:T(8,128)S(1)}, u32[]{:S(2)}, u32[]{:S(2)}) collective-permute-start(f32[16,1024]{1,0:T(8,128)S(1)} %pad_maximum_fusion), channel_id=1, source_target_pairs={{0,16},{1,17},{2,18},{3,19},{4,20},{5,21},{6,22},{7,23},{8,24},{9,... | collective-permute-start | bytes 196616 | tf_op jit(solution)/shard_map/ppermute | solution.py:1102
  357.5 38.0 %collective-permute-start.2 = (bf16[256,1024]{1,0:T(8,128)(2,1)S(1)}, bf16[256,1024]{1,0:T(8,128)(2,1)S(1)}, u32[]{:S(2)}, u32[]{:S(2)}) collective-permute-start(bf16[256,1024]{1,0:T(8,128)(2,1)S(1)} %get-tuple-element.37), channel_id=1, source_target_pairs={{1,0},{3,2},{5,4},{7,6},{9,8},{11,10},{13,12},{15,14},{16,1},{18,3... | collective-permute-start | bytes 1572872 | tf_op jit(solution)/shard_map/ppermute | solution.py:1102
  358.8 11.8 %collective-permute-start.14 = (f32[16,1024]{1,0:T(8,128)S(1)}, f32[16,1024]{1,0:T(8,128)S(1)}, u32[]{:S(2)}, u32[]{:S(2)}) collective-permute-start(f32[16,1024]{1,0:T(8,128)S(1)} %fusion), channel_id=1, source_target_pairs={{0,1},{1,0},{2,3},{3,2},{4,5},{5,4},{6,7},{7,6},{8,9},{9,8},{10,11... | collective-permute-start | bytes 196616 | tf_op jit(solution)/shard_map/ppermute | solution.py:1102
  361.6 10.0 %collective-permute-start.9 = (f32[16,1024]{1,0:T(8,128)S(1)}, f32[16,1024]{1,0:T(8,128)S(1)}, u32[]{:S(2)}, u32[]{:S(2)}) collective-permute-start(f32[16,1024]{1,0:T(8,128)S(1)} %fusion.1), channel_id=1, source_target_pairs={{0,1},{1,0},{2,3},{3,2},{4,5},{5,4},{6,7},{7,6},{8,9},{9,8},{10,11... | collective-permute-start | bytes 196616 | tf_op jit(solution)/shard_map/ppermute | solution.py:1102
  370.7 4.3 %collective-permute-start.15 = (f32[16,1024]{1,0:T(8,128)S(1)}, f32[16,1024]{1,0:T(8,128)S(1)}, u32[]{:S(2)}, u32[]{:S(2)}) collective-permute-start(f32[16,1024]{1,0:T(8,128)S(1)} %add.60), channel_id=1, source_target_pairs={{0,2},{1,3},{2,0},{3,1},{4,6},{5,7},{6,4},{7,5},{8,10},{9,11},{10,... | collective-permute-start | bytes 196616 | tf_op jit(solution)/shard_map/ppermute | solution.py:1102
  371.6 5.0 %collective-permute-start.10 = (f32[16,1024]{1,0:T(8,128)S(1)}, f32[16,1024]{1,0:T(8,128)S(1)}, u32[]{:S(2)}, u32[]{:S(2)}) collective-permute-start(f32[16,1024]{1,0:T(8,128)S(1)} %add.55), channel_id=1, source_target_pairs={{0,2},{1,3},{2,0},{3,1},{4,6},{5,7},{6,4},{7,5},{8,10},{9,11},{10,... | collective-permute-start | bytes 196616 | tf_op jit(solution)/shard_map/ppermute | solution.py:1102
  375.0 5.0 %collective-permute-start.16 = (f32[16,1024]{1,0:T(8,128)S(1)}, f32[16,1024]{1,0:T(8,128)S(1)}, u32[]{:S(2)}, u32[]{:S(2)}) collective-permute-start(f32[16,1024]{1,0:T(8,128)S(1)} %add.61), channel_id=1, source_target_pairs={{0,4},{1,5},{2,6},{3,7},{4,0},{5,1},{6,2},{7,3},{8,12},{9,13},{10,... | collective-permute-start | bytes 196616 | tf_op jit(solution)/shard_map/ppermute | solution.py:1102
  376.6 5.5 %collective-permute-start.11 = (f32[16,1024]{1,0:T(8,128)S(1)}, f32[16,1024]{1,0:T(8,128)S(1)}, u32[]{:S(2)}, u32[]{:S(2)}) collective-permute-start(f32[16,1024]{1,0:T(8,128)S(1)} %add.56), channel_id=1, source_target_pairs={{0,4},{1,5},{2,6},{3,7},{4,0},{5,1},{6,2},{7,3},{8,12},{9,13},{10,... | collective-permute-start | bytes 196616 | tf_op jit(solution)/shard_map/ppermute | solution.py:1102
  380.1 5.9 %collective-permute-start.17 = (f32[16,1024]{1,0:T(8,128)S(1)}, f32[16,1024]{1,0:T(8,128)S(1)}, u32[]{:S(2)}, u32[]{:S(2)}) collective-permute-start(f32[16,1024]{1,0:T(8,128)S(1)} %add.62), channel_id=1, source_target_pairs={{0,8},{1,9},{2,10},{3,11},{4,12},{5,13},{6,14},{7,15},{8,0},{9,1},... | collective-permute-start | bytes 196616 | tf_op jit(solution)/shard_map/ppermute | solution.py:1102
  382.2 5.2 %collective-permute-start.12 = (f32[16,1024]{1,0:T(8,128)S(1)}, f32[16,1024]{1,0:T(8,128)S(1)}, u32[]{:S(2)}, u32[]{:S(2)}) collective-permute-start(f32[16,1024]{1,0:T(8,128)S(1)} %add.57), channel_id=1, source_target_pairs={{0,8},{1,9},{2,10},{3,11},{4,12},{5,13},{6,14},{7,15},{8,0},{9,1},... | collective-permute-start | bytes 196616 | tf_op jit(solution)/shard_map/ppermute | solution.py:1102
  386.0 12.4 %collective-permute-start = (bf16[256,1024]{1,0:T(8,128)(2,1)S(1)}, bf16[256,1024]{1,0:T(8,128)(2,1)S(1)}, u32[]{:S(2)}, u32[]{:S(2)}) collective-permute-start(bf16[256,1024]{1,0:T(8,128)(2,1)S(1)} %get-tuple-element.37), channel_id=1, source_target_pairs={{0,0},{2,2},{4,4},{6,6},{8,8},{10,10},{12,12},{14,14},{17,1},{19,3... | collective-permute-start | bytes 1572872 | tf_op jit(solution)/shard_map/ppermute | solution.py:1102
  387.4 11.0 %collective-permute-start.7 = (bf16[256,1024]{1,0:T(8,128)(2,1)S(1)}, bf16[256,1024]{1,0:T(8,128)(2,1)S(1)}, u32[]{:S(2)}, u32[]{:S(2)}) collective-permute-start(bf16[256,1024]{1,0:T(8,128)(2,1)S(1)} %get-tuple-element.34), channel_id=1, source_target_pairs={{1,16},{3,18},{5,20},{7,22},{9,24},{11,26},{13,28},{15,30},{16,17}... | collective-permute-start | bytes 1572872 | tf_op jit(solution)/shard_map/ppermute | solution.py:1102
  388.1 10.3 %collective-permute-start.5 = (bf16[256,1024]{1,0:T(8,128)(2,1)S(1)}, bf16[256,1024]{1,0:T(8,128)(2,1)}, u32[]{:S(2)}, u32[]{:S(2)}) collective-permute-start(bf16[256,1024]{1,0:T(8,128)(2,1)S(1)} %get-tuple-element.34), channel_id=1, source_target_pairs={{0,16},{2,18},{4,20},{6,22},{8,24},{10,26},{12,28},{14,30},{17,17}... | collective-permute-start | bytes 1572872 | tf_op jit(solution)/shard_map/ppermute | solution.py:1102
  394.0 11.1 %collective-permute-start.6 = (bf16[256,1024]{1,0:T(8,128)(2,1)S(1)}, bf16[256,1024]{1,0:T(8,128)(2,1)S(1)}, u32[]{:S(2)}, u32[]{:S(2)}) collective-permute-start(bf16[256,1024]{1,0:T(8,128)(2,1)S(1)} %get-tuple-element.35), channel_id=1, source_target_pairs={{1,0},{3,2},{5,4},{7,6},{9,8},{11,10},{13,12},{15,14},{16,1},{18,3... | collective-permute-start | bytes 1572872 | tf_op jit(solution)/shard_map/ppermute | solution.py:1102
  395.5 0.8 copy-start.2
  396.3 8.7 %collective-permute-start.4 = (bf16[256,1024]{1,0:T(8,128)(2,1)S(1)}, bf16[256,1024]{1,0:T(8,128)(2,1)}, u32[]{:S(2)}, u32[]{:S(2)}) collective-permute-start(bf16[256,1024]{1,0:T(8,128)(2,1)S(1)} %get-tuple-element.35), channel_id=1, source_target_pairs={{0,0},{2,2},{4,4},{6,6},{8,8},{10,10},{12,12},{14,14},{17,1},{19,3... | collective-permute-start | bytes 1572872 | tf_op jit(solution)/shard_map/ppermute | solution.py:1102

commit v3 on v2

--- a/solution.py
+++ b/solution.py
@@ -500,31 +500,38 @@
         self.sent = [one for one in self.sent if one is not copy]
 
 
-WIRES = 40
+WIRES = 96
 
 
 def step_kernel(
     block,
     model,
-    x_mine,
-    x_other,
-    cot_mine,
-    cot_other,
-    seg_col,
-    seg_row,
-    small,
+    planes,
+    x_rows,
+    cot_rows,
+    seg_cols,
+    seg_rows,
+    gain_a,
+    gain_m,
+    downs_t,
+    up_q,
+    up_v,
     wq,
-    up,
     wo,
     fc,
     proj,
+    act_out,
+    grad_out,
+    sums_out,
     act,
     grad,
-    down_sums,
-    up_sums,
     xb,
     cb,
+    seg_col,
+    seg_row,
     sm,
+    up,
+    pad,
     wq_all,
     up_all,
     wo_all,
@@ -540,8 +547,6 @@
     part_out,
     part_in,
     own_sum,
-    far_up,
-    grad_mid,
     do_in,
     dqkv,
     dk_acc,
@@ -550,17 +555,25 @@
     c_in,
     y_out,
     y_in,
+    down_sums,
+    up_sums,
+    total_out,
+    total_in,
     wire_send,
     wire_recv,
     row_send,
     row_recv,
     wq_send,
     wq_recv,
+    wq_half,
     local_sem,
     o_send,
     o_recv,
+    place_send,
+    place_recv,
 ):
     c = lax.axis_index("section")
+    z = lax.axis_index("dp")
     t = lax.axis_index("tensor")
     y, x = lax.div(t, 2), lax.rem(t, 2)
     over_x, over_y = 2 * y + (1 - x), 2 * (1 - y) + x
@@ -569,15 +582,28 @@
     to_c, to_x, to_y = {"section": 1 - c}, {"tensor": over_x}, {"tensor": over_y}
     to_xc = {"section": 1 - c, "tensor": over_x}
     to_yc = {"section": 1 - c, "tensor": over_y}
+    to_zs = []
+    bit = 1
+    while bit < planes:
+        up_bit = lax.rem(lax.div(z, bit), 2)
+        to_zs.append({"dp": z + bit - 2 * bit * up_bit})
+        bit *= 2
+    to_z = to_zs[0]
+    odd = lax.rem(z, 2)
     here = c == x
     wires = Wires(wire_send, wire_recv)
     width = wq.shape[2]
     factor = 8.0
 
     barrier = pltpu.get_barrier_semaphore()
-    for peer in (to_c, to_x, to_y, to_xc, to_yc):
+    peers = [to_c, to_x, to_y, to_xc, to_yc, *to_zs]
+    for peer in peers:
         pl.semaphore_signal(barrier, inc=1, device_id=peer, device_id_type=MESH)
-    pl.semaphore_wait(barrier, 5)
+    pl.semaphore_wait(barrier, len(peers))
+
+    def part(which, count):
+        first = odd if which == 0 else 1 - odd
+        return pl.ds(pl.multiple_of(first * (count // 2), count // 2), count // 2)
 
     def row_copy(source, target, k):
         return pltpu.make_async_remote_copy(
@@ -589,28 +615,65 @@
             device_id_type=MESH,
         )
 
-    sm[c] = small[...]
-    small_copy = wires.copy(small, sm.at[c], to_c)
-    small_copy.start()
-    x_copy = row_copy(x_other, xb, 0)
+    x_copy = row_copy(x_rows.at[1 - x], xb, 0)
 
     @pl.when(here)
     def _():
         x_copy.start()
-        xb[...] = x_mine[...]
-
-    def wq_pair(k, where):
+        pltpu.make_async_copy(x_rows.at[x], xb, row_recv.at[0]).start()
+
+    pad[...] = jnp.zeros_like(pad)
+    pad[0:4] = up_q[...].astype(F32)
+    up[0] = pad[...].astype(BF16)
+    pad[0:4] = jnp.zeros((4, width), F32)
+    pad[4:8] = up_v[...].astype(F32)
+    up[1] = pad[...].astype(BF16)
+
+    def wq_twin():
         return [
             pltpu.make_async_remote_copy(
                 src_ref=source,
                 dst_ref=target.at[c],
-                send_sem=wq_send.at[k, j],
+                send_sem=wq_send.at[0, j],
                 recv_sem=wq_recv.at[c, j],
-                device_id=where,
+                device_id=to_c,
                 device_id_type=MESH,
             )
             for j, (source, target) in enumerate(((wq, wq_all), (up, up_all)))
         ]
+
+    def wq_over_x():
+        cut = part(0, model)
+        where = {"section": x, "tensor": over_x}
+        return [
+            pltpu.make_async_remote_copy(
+                src_ref=wq.at[:, cut],
+                dst_ref=wq_all.at[c, :, cut],
+                send_sem=wq_send.at[1, 0],
+                recv_sem=wq_half.at[c, 0],
+                device_id=where,
+                device_id_type=MESH,
+            ),
+            pltpu.make_async_remote_copy(
+                src_ref=up,
+                dst_ref=up_all.at[c],
+                send_sem=wq_send.at[1, 1],
+                recv_sem=wq_recv.at[c, 1],
+                device_id=where,
+                device_id_type=MESH,
+            ),
+        ]
+
+    def wq_over_z(layer):
+        cut = part(0, model)
+        return pltpu.make_async_remote_copy(
+            src_ref=wq_all.at[layer, :, cut],
+            dst_ref=wq_all.at[layer, :, cut],
+            send_sem=wq_send.at[2, layer],
+            recv_sem=wq_half.at[layer, 1],
+            device_id=to_z,
+            device_id_type=MESH,
+        )
 
     def wq_local(layer):
         return [
@@ -619,7 +682,7 @@
         ]
 
     def send_wq():
-        for copy in wq_pair(1, {"section": x, "tensor": over_x}):
+        for copy in wq_over_x():
             copy.start()
 
         @pl.when(here)
@@ -629,19 +692,49 @@
 
         @pl.when(jnp.logical_not(here))
         def _():
-            for copy in wq_pair(0, to_c):
+            for copy in wq_twin():
                 copy.start()
 
+    def half_wait(layer, k):
+        cut = part(k, model)
+        pltpu.make_async_copy(wq.at[:, cut], wq_all.at[layer, :, cut], wq_half.at[layer, k]).wait()
+
+    def pass_wq(layer):
+        @pl.when(jnp.logical_not(here))
+        def _():
+            half_wait(layer, 0)
+            wq_over_z(layer).start()
+
+    def arrived_wq(layer):
+        whole, small = wq_local(layer)
+        small.wait()
+        pl.when(here)(whole.wait)
+
+        @pl.when(jnp.logical_not(here))
+        def _():
+            half_wait(layer, 1)
+
     def sent_wq():
-        for copy in wq_pair(1, to_x):
+        for copy in wq_over_x():
             copy.wait_send()
 
         @pl.when(jnp.logical_not(here))
         def _():
-            for copy in wq_pair(0, to_c):
+            for copy in wq_twin():
                 copy.wait_send()
+            for layer in range(2):
+                wq_over_z(layer).wait_send()
 
     pl.when(c == 0)(send_wq)
+
+    sm[c, 0:1] = gain_a[...]
+    sm[c, 8:9] = gain_m[...]
+    sm[c, 16:24] = downs_t[...].astype(F32)
+    sm[c, 24:32] = jnp.zeros((8, model), F32)
+    small_copy = wires.copy(sm.at[c], sm.at[c], to_c)
+    small_copy.start()
+    seg_row[...] = seg_rows[pl.ds(x, 1), :]
+    seg_col[...] = jnp.where(x == 0, seg_cols[:, 0:1], seg_cols[:, 1:2])
 
     locals_ = [
         pltpu.make_async_copy(source, target, local_sem.at[k])
@@ -649,51 +742,145 @@
             ((fc, ff.at[c, 0, 0]), (proj, ff.at[c, 1, 0]), (wo, wo_all.at[c, t]))
         )
     ]
+    ff_cut, ff_rest = part(0, model), part(1, model)
+    ff_twin = [wires.copy(one, ff.at[c, k, 0], to_c) for k, one in enumerate((fc, proj))]
+    ff_y = [
+        wires.copy(one.at[ff_cut], ff.at[c, k, 1, ff_cut], to_y) for k, one in enumerate((fc, proj))
+    ]
+    ff_z = [wires.copy(ff.at[c, k, 1, ff_cut], ff.at[c, k, 1, ff_cut], to_z) for k in range(2)]
+    ff_c = [
+        [wires.copy(ff.at[c, k, 1, cut], ff.at[c, k, 1, cut], to_c) for cut in (ff_cut, ff_rest)]
+        for k in range(2)
+    ]
+
+    def on_core(layer, action):
+        pl.when(c == layer)(action)
+
+    def start_ff(layer):
+        @pl.when(c == layer)
+        def _():
+            for copy in ff_y:
+                copy.start()
+
+    def pass_ff_y(layer, k):
+        @pl.when(c == layer)
+        def _():
+            ff_y[k].wait_recv()
+            ff_z[k].start()
+            ff_c[k][0].start()
+
+    def pass_ff_z(layer, k):
+        @pl.when(c == layer)
+        def _():
+            ff_z[k].wait_recv()
+            ff_c[k][1].start()
+
+    def arrived_ff(layer):
+        @pl.when(c != layer)
+        def _():
+            for pair in ff_c:
+                for copy in pair:
+                    copy.wait_recv()
+
+    corner = 2 * (1 - y) + (1 - x)
+    wo_cut = part(0, width)
+    quart = width // 4
+    wo_low = pl.ds(pl.multiple_of(odd * (width // 2), quart), quart)
+    wo_high = pl.ds(pl.multiple_of(odd * (width // 2) + quart, quart), quart)
+
+    def wo_same(q, cut, where):
+        if cut is None:
+            return wires.copy(wo_all.at[c, q], wo_all.at[c, q], where)
+        return wires.copy(wo_all.at[c, q, cut], wo_all.at[c, q, cut], where)
+
+    wo_twin = wires.copy(wo, wo_all.at[c, t], to_c)
+    wo_x = wires.copy(wo.at[wo_cut], wo_all.at[c, t, wo_cut], to_x)
+    wo_y = wires.copy(wo.at[wo_cut], wo_all.at[c, t, wo_cut], to_y)
+    wo_dy = wo_same(over_x, wo_low, to_y)
+    wo_dx = wo_same(over_y, wo_high, to_x)
+    wo_z = [wo_same(q, wo_cut, to_z) for q in (over_x, over_y, corner)]
+    wo_c = [wo_same(q, None, to_c) for q in (over_x, over_y, corner)]
+
+    def start_wo(layer):
+        @pl.when(c == layer)
+        def _():
+            wo_x.start()
+            wo_y.start()
+
+    def pass_wo(layer, stage):
+        @pl.when(c == layer)
+        def _():
+            if stage == 0:
+                wo_x.wait_recv()
+                wo_dy.start()
+                wo_z[0].start()
+                wo_y.wait_recv()
+                wo_dx.start()
+                wo_z[1].start()
+            if stage == 1:
+                wo_dy.wait_recv()
+                wo_dx.wait_recv()
+                wo_z[2].start()
+            if stage == 2:
+                for came, onward in zip(wo_z, wo_c):
+                    came.wait_recv()
+                    onward.start()
+
+    def arrived_wo(layer):
+        @pl.when(c == layer)
+        def _():
+            locals_[2].wait()
+
+        @pl.when(c != layer)
+        def _():
+            wo_twin.wait_recv()
+            for copy in wo_c:
+                copy.wait_recv()
+
+    start_ff(0)
+    start_wo(0)
     for copy in locals_:
         copy.start()
-    ff_twin = [wires.copy(one, ff.at[c, k, 0], to_c) for k, one in enumerate((fc, proj))]
-    ff_y = [wires.copy(one, ff.at[c, k, 1], to_y) for k, one in enumerate((fc, proj))]
-    ff_y_twin = [wires.copy(ff.at[c, k, 1], ff.at[c, k, 1], to_c) for k in range(2)]
-    wo_twin = wires.copy(wo, wo_all.at[c, t], to_c)
-    wo_x = wires.copy(wo, wo_all.at[c, t], to_x)
-    wo_y = wires.copy(wo, wo_all.at[c, t], to_y)
-    half = width // 2
-    wo_dy = wires.copy(
-        wo_all.at[c, over_x, pl.ds(0, half)], wo_all.at[c, over_x, pl.ds(0, half)], to_y
-    )
-    wo_dx = wires.copy(
-        wo_all.at[c, over_y, pl.ds(half, half)], wo_all.at[c, over_y, pl.ds(half, half)], to_x
-    )
-    corner = 2 * (1 - y) + (1 - x)
-    wo_twins = [
-        wires.copy(wo_all.at[c, q], wo_all.at[c, q], to_c) for q in (over_x, over_y, corner)
-    ]
-
-    def start_ff(layer):
-        @pl.when(c == layer)
-        def _():
-            for copy in ff_y:
-                copy.start()
-
-    def pass_ff(layer):
-        @pl.when(c == layer)
-        def _():
-            for copy, onward in zip(ff_y, ff_y_twin):
-                copy.wait_recv()
-                onward.start()
-
-        @pl.when(c != layer)
-        def _():
-            for onward in ff_y_twin:
-                onward.wait_recv()
-
-    start_ff(0)
     for copy in ff_twin + [wo_twin]:
         copy.start()
 
-    def arrived_wq(layer):
-        for copy in wq_local(layer):
-            copy.wait()
+    def place_copy(kind, layer, source, target):
+        return pltpu.make_async_remote_copy(
+            src_ref=source,
+            dst_ref=target.at[x],
+            send_sem=place_send.at[kind, layer],
+            recv_sem=place_recv.at[kind, x],
+            device_id={"section": layer, "tensor": mine},
+            device_id_type=MESH,
+        )
+
+    def place(kind, layer, source, target):
+        stays = jnp.logical_and(here, c == layer)
+
+        @pl.when(stays)
+        def _():
+            target[x] = source[...]
+
+        @pl.when(jnp.logical_not(stays))
+        def _():
+            place_copy(kind, layer, source, target).start()
+
+    def placed(kind, source, target):
+        for layer in range(2):
+            stays = jnp.logical_and(here, c == layer)
+
+            @pl.when(jnp.logical_not(stays))
+            def _():
+                place_copy(kind, layer, source.at[layer], target).wait_send()
+
+        for slot in range(2):
+            came = jnp.logical_not(jnp.logical_and(here, x == slot))
+
+            @pl.when(came)
+            def _():
+                pltpu.make_async_copy(
+                    source.at[0], target.at[slot], place_recv.at[kind, slot]
+                ).wait()
 
     def qkv_block(layer, b):
         normed = rows[layer, b]
@@ -780,11 +967,17 @@
             total = term if total is None else total + term
         return total
 
-    @pl.when(jnp.logical_not(here))
-    def _():
-        x_copy.wait_recv()
-
+    pltpu.make_async_copy(x_rows.at[x], xb, row_recv.at[0]).wait()
     small_copy.wait_recv()
+    cot_copies = [
+        row_copy(cot_rows.at[1 - x], cb.at[0], 1),
+        row_copy(cot_rows.at[x], cb.at[1], 2),
+    ]
+
+    cot_local = [
+        pltpu.make_async_copy(cot_rows.at[x], cb.at[0], row_recv.at[1]),
+        pltpu.make_async_copy(cot_rows.at[1 - x], cb.at[1], row_recv.at[2]),
+    ]
 
     for layer in range(2):
         source = xb if layer == 0 else act.at[0]
@@ -795,35 +988,49 @@
         row_yc = wires.copy(rows.at[layer, far], rows.at[layer, far], to_c)
         row_y.start()
         row_c.start()
+        if layer == 0:
+            pass_wq(0)
+            pass_wo(0, 0)
+        else:
+            place(0, 0, act.at[0], act_out)
+
+            @pl.when(here)
+            def _():
+                for copy in cot_copies:
+                    copy.start()
+                for copy in cot_local:
+                    copy.start()
+
+            pass_ff_z(1, 0)
+            pass_wo(1, 2)
         arrived_wq(layer)
         if layer == 0:
-            for copy in (wo_x, wo_y):
-                copy.start()
+            pl.when(c == 1)(send_wq)
         qkv_block(layer, mine)
         row_c.wait_recv()
         qkv_block(layer, twin)
+        if layer == 0:
+            pass_ff_y(0, 0)
         row_y.wait_recv()
         row_yc.start()
         qkv_block(layer, far)
         row_yc.wait_recv()
         qkv_block(layer, far_twin)
+        if layer == 0:
+            pass_wo(0, 1)
         for i in range(4):
             attend(layer, i)
             send_piece(i, o_in, layer)
+            if layer == 0 and i == 0:
+                pass_ff_y(0, 1)
+            if layer == 0 and i == 2:
+                pass_ff_z(0, 0)
+                pass_wo(0, 2)
         if layer == 0:
-            locals_[2].wait()
-            wo_x.wait_recv()
-            wo_dy.start()
-            wo_twins[0].start()
-            wo_y.wait_recv()
-            wo_dx.start()
-            wo_twins[1].start()
-            wo_dy.wait_recv()
-            wo_dx.wait_recv()
-            wo_twins[2].start()
-            wo_twin.wait_recv()
-            for copy in wo_twins:
-                copy.wait_recv()
+            pass_wq(1)
+        else:
+            pass_ff_z(1, 1)
+        arrived_wo(layer)
         wait_pieces(o_in, layer)
         stream = source[...].astype(F32)
         for q in range(4):
@@ -834,56 +1041,52 @@
         norm_x = wires.copy(norm2.at[0], norm2.at[1], to_x)
         norm_x.start()
         if layer == 0:
+            start_ff(1)
+            start_wo(1)
+            pass_ff_z(0, 1)
             for copy in locals_[:2]:
                 copy.wait()
             for copy in ff_twin:
                 copy.wait_recv()
         own_sum[...] = hidden_half(layer, 0, norm2[0], 0)
+        arrived_ff(layer)
+        own_sum[...] += hidden_half(layer, 0, norm2[0], 1)
         norm_x.wait_recv()
-        away = hidden_half(layer, 1, norm2[1], 0)
-        pass_ff(layer)
-        away = away + hidden_half(layer, 1, norm2[1], 1)
+        away = hidden_half(layer, 1, norm2[1], 0) + hidden_half(layer, 1, norm2[1], 1)
         part_out[...] = away.astype(BF16)
         part_x = wires.copy(part_out, part_in.at[0], to_x)
         part_x.start()
         if layer == 0:
-            start_ff(1)
-            pl.when(c == 1)(send_wq)
-        stream = middle[layer] + own_sum[...] + hidden_half(layer, 0, norm2[0], 1)
+            pass_ff_y(1, 0)
+            pass_wo(1, 0)
+        stream = middle[layer] + own_sum[...]
+        if layer == 0:
+            pass_ff_y(1, 1)
+            pass_wo(1, 1)
         part_x.wait()
         wires.forget(part_x)
         norm_x.wait_send()
         wires.forget(norm_x)
         act[layer] = (stream + part_in[0].astype(F32)).astype(BF16)
-        if layer == 0:
-            cot_copies = [row_copy(cot_other, cb.at[0], 1), row_copy(cot_mine, cb.at[1], 2)]
-
-            @pl.when(here)
-            def _():
-                for copy in cot_copies:
-                    copy.start()
-                cb[0] = cot_mine[...]
-                cb[1] = cot_other[...]
-
-    @pl.when(jnp.logical_not(here))
-    def _():
-        for copy in cot_copies:
-            copy.wait_recv()
+
+    for copy in cot_local:
+        copy.wait()
 
     for layer in (1, 0):
         upstream = cb[0] if layer == 1 else grad[1]
         if layer == 1:
             away = hidden_back(layer, 1, cb[1], 0) + hidden_back(layer, 1, cb[1], 1)
         else:
-            up_x = wires.copy(grad.at[1], far_up, to_x)
+            up_x = wires.copy(grad.at[1], norm2.at[1], to_x)
             up_x.start()
             own_sum[...] = hidden_back(layer, 0, upstream, 0) + hidden_back(layer, 0, upstream, 1)
             up_x.wait_recv()
-            away = hidden_back(layer, 1, far_up[...], 0) + hidden_back(layer, 1, far_up[...], 1)
+            away = hidden_back(layer, 1, norm2[1], 0) + hidden_back(layer, 1, norm2[1], 1)
         part_out[...] = away.astype(BF16)
         part_x = wires.copy(part_out, part_in.at[1], to_x)
         part_x.start()
         if layer == 1:
+            place(0, 1, act.at[1], act_out)
             own_sum[...] = hidden_back(layer, 0, upstream, 0) + hidden_back(layer, 0, upstream, 1)
         unit, inverse = norm_stats(middle[layer])
         part_x.wait()
@@ -892,13 +1095,15 @@
         grad_middle = upstream.astype(F32) + normalize_back(
             grad_norm, unit, inverse, sm[layer, 8:9, :]
         )
-        grad_mid[...] = grad_middle
+        own_sum[...] = grad_middle
         grad_b = grad_middle.astype(BF16)
         for q in range(4):
             made = dot_nt(grad_b, wo_all[layer, q]).astype(BF16)
             o_out[q, 0] = made[:, :128]
             o_out[q, 1] = made[:, 128:]
             send_piece(q, do_in, 2 + layer)
+        if layer == 0:
+            place(1, 1, grad.at[1], grad_out)
         wait_pieces(do_in, 2 + layer)
 
         def back_pair(pair, carry):
@@ -953,12 +1158,12 @@
             to_down = dot_tn(low_b, rows[layer, b])
             to_up = [factor * dot_tn(kept, parts[0]), factor * dot_tn(kept, parts[2])]
             if first:
-                down_sums[layer] = to_down
-                up_sums[layer, 0], up_sums[layer, 1] = to_up
+                down_sums[...] = to_down
+                up_sums[0], up_sums[1] = to_up
             else:
-                down_sums[layer] += to_down
-                up_sums[layer, 0] += to_up[0]
-                up_sums[layer, 1] += to_up[1]
+                down_sums[...] += to_down
+                up_sums[0] += to_up[0]
+                up_sums[1] += to_up[1]
             return term
 
         c_far = wires.copy(c_out.at[0], c_in.at[0], to_c)
@@ -973,14 +1178,35 @@
         c_out[1] = block_grad(twin, False).astype(BF16)
         c_near.start()
         term = block_grad(mine, False)
-        c_near.wait_recv()
-        term = term + c_in[1].astype(F32)
-        source = xb if layer == 0 else act.at[0]
-        unit, inverse = norm_stats(source[...].astype(F32))
+        total_out[layer, 0, 0:8] = down_sums[0:8]
+        total_out[layer, 0, 8:16] = jnp.zeros((8, model), F32)
+        low_rows = lax.broadcasted_iota(jnp.int32, (8, width), 0) < 4
+        total_out[
+            layer, 0, 8:16, pl.ds(pl.multiple_of(mine * width, width), width)
+        ] = jnp.where(low_rows, up_sums[0, 0:8], up_sums[1, 0:8])
+        hops = [to_c, to_x, to_y, *to_zs]
+        for k, peer in enumerate(hops):
+            hop = wires.copy(total_out.at[layer, k], total_in.at[layer, k], peer)
+            hop.start()
+            if k == 0:
+                c_near.wait_recv()
+                term = term + c_in[1].astype(F32)
+                source = xb if layer == 0 else act.at[0]
+                unit, inverse = norm_stats(source[...].astype(F32))
+            hop.wait_recv()
+            summed = total_out[layer, k] + total_in[layer, k]
+            if k + 1 < len(hops):
+                total_out[layer, k + 1] = summed
+            else:
+
+                @pl.when(c == layer)
+                def _():
+                    sums_out[...] = summed
+
         y_far.wait_recv()
         grad_norm = term + y_in[...].astype(F32)
         grad[layer] = (
-            grad_mid[...] + normalize_back(grad_norm, unit, inverse, sm[layer, 0:1, :])
+            own_sum[...] + normalize_back(grad_norm, unit, inverse, sm[layer, 0:1, :])
         ).astype(BF16)
         for copy in (c_far, c_near, y_far):
             copy.wait_send()
@@ -992,29 +1218,38 @@
         for copy in cot_copies:
             copy.wait_send()
 
+    place(1, 0, grad.at[0], grad_out)
     sent_wq()
     for copy in wires.sent:
         copy.wait_send()
-
-
-def step_call(block, model, width, rank, operands):
+    placed(0, act, act_out)
+    placed(1, grad, grad_out)
+
+
+def step_call(block, model, width, planes, operands):
     slots = 4 * block
+    hops = 3 + (planes - 1).bit_length()
     in_vmem = pl.BlockSpec(memory_space=pltpu.VMEM)
     in_hbm = pl.BlockSpec(memory_space=pl.ANY)
     return pl.pallas_call(
-        functools.partial(step_kernel, block, model),
+        functools.partial(step_kernel, block, model, planes),
         out_shape=(
             jax.ShapeDtypeStruct((2, block, model), BF16),
             jax.ShapeDtypeStruct((2, block, model), BF16),
-            jax.ShapeDtypeStruct((2, 16, model), F32),
-            jax.ShapeDtypeStruct((2, 2, 16, width), F32),
+            jax.ShapeDtypeStruct((16, model), F32),
         ),
-        in_specs=[in_vmem] * 7 + [in_hbm] * 5,
-        out_specs=[in_vmem] * 4,
+        in_specs=[in_hbm] * 2 + [in_vmem] * 7 + [in_hbm] * 4,
+        out_specs=[in_vmem] * 3,
         scratch_shapes=[
+            pltpu.VMEM((2, block, model), BF16),
+            pltpu.VMEM((2, block, model), BF16),
             pltpu.VMEM((block, model), BF16),
             pltpu.VMEM((2, block, model), BF16),
+            pltpu.VMEM((slots, 1), jnp.int32),
+            pltpu.VMEM((1, slots), jnp.int32),
             pltpu.VMEM((2, 32, model), F32),
+            pltpu.VMEM((2, 16, width), BF16),
+            pltpu.VMEM((16, width), F32),
             pltpu.VMEM((2, 3, model, width), BF16),
             pltpu.VMEM((2, 2, 16, width), BF16),
             pltpu.VMEM((2, 4, width, model), BF16),
@@ -1030,8 +1265,6 @@
             pltpu.VMEM((block, model), BF16),
             pltpu.VMEM((2, block, model), BF16),
             pltpu.VMEM((block, model), F32),
-            pltpu.VMEM((block, model), BF16),
-            pltpu.VMEM((block, model), F32),
             pltpu.VMEM((4, 2, block, 128), BF16),
             pltpu.VMEM((3, 2, slots, 128), BF16),
             pltpu.VMEM((slots, 128), F32),
@@ -1040,38 +1273,27 @@
             pltpu.VMEM((2, block, model), BF16),
             pltpu.VMEM((block, model), BF16),
             pltpu.VMEM((block, model), BF16),
+            pltpu.VMEM((16, model), F32),
+            pltpu.VMEM((2, 16, width), F32),
+            pltpu.VMEM((2, hops, 16, model), F32),
+            pltpu.VMEM((2, hops, 16, model), F32),
             pltpu.SemaphoreType.DMA((WIRES,)),
             pltpu.SemaphoreType.DMA((WIRES,)),
             pltpu.SemaphoreType.DMA((3,)),
             pltpu.SemaphoreType.DMA((3,)),
+            pltpu.SemaphoreType.DMA((3, 2)),
             pltpu.SemaphoreType.DMA((2, 2)),
             pltpu.SemaphoreType.DMA((2, 2)),
             pltpu.SemaphoreType.DMA((3,)),
             pltpu.SemaphoreType.DMA((4,)),
             pltpu.SemaphoreType.DMA((4, 4)),
+            pltpu.SemaphoreType.DMA((2, 2)),
+            pltpu.SemaphoreType.DMA((2, 2)),
         ],
         compiler_params=pltpu.CompilerParams(
-            collective_id=0, has_side_effects=True, vmem_limit_bytes=61 * 1024 * 1024
+            collective_id=0, has_side_effects=True, vmem_limit_bytes=62 * 1024 * 1024
         ),
     )(*operands)
-
-
-ROUTE_AXES = ("section", "dp", "tensor")
-
-
-def route(planes, rule):
-    pairs = []
-    for c in range(2):
-        for z in range(planes):
-            for y in range(2):
-                for x in range(2):
-                    target = rule(c, z, y, x)
-                    if target is not None:
-                        tc, tz, ty, tx = target
-                        pairs.append(
-                            ((c * planes + z) * 4 + 2 * y + x, (tc * planes + tz) * 4 + 2 * ty + tx)
-                        )
-    return pairs
 
 
 def fast_body(
@@ -1090,99 +1312,34 @@
     w_fc,
     w_proj,
 ):
-    core = lax.axis_index("section")
-    place = lax.axis_index("tensor")
-    y, x = place // 2, place % 2
     block, _, model = inputs.shape
     width = joint_projection_weight.shape[3]
     rank = query_down_factor.shape[2]
-    core_0, x_0 = core == 0, x == 0
-
-    def sent(value, rule):
-        return lax.ppermute(value, ROUTE_AXES, route(planes, rule))
-
-    def both_rows(array):
-        return (
-            jnp.where(x_0, array[:, 0], array[:, 1]),
-            jnp.where(x_0, array[:, 1], array[:, 0]),
-        )
-
-    segment_row = jnp.where(x_0, segments[0], segments[1])
-    blank = jnp.zeros((7, model), F32)
-    small = jnp.concatenate(
-        [
-            gain_attn,
-            blank,
-            gain_mlp,
-            blank,
-            query_down_factor[0].T.astype(F32),
-            value_down_factor[0].T.astype(F32),
-            jnp.zeros((16 - 2 * rank, model), F32),
-        ],
-        axis=0,
-    )
-    ups = jnp.stack(
-        [
-            jnp.pad(query_up_factor[0], ((0, 16 - rank), (0, 0))),
-            jnp.pad(value_up_factor[0], ((rank, 16 - 2 * rank), (0, 0))),
-        ]
-    )
-    acts, grads, down_sums, up_sums = step_call(
+    downs = jnp.concatenate([query_down_factor[0], value_down_factor[0]], axis=1)
+    acts, grads, total = step_call(
         block,
         model,
         width,
-        rank,
+        planes,
         (
-            *both_rows(inputs),
-            *both_rows(cotangent),
-            segment_row[:, None],
-            segment_row[None, :],
-            small,
+            jnp.swapaxes(inputs, 0, 1),
+            jnp.swapaxes(cotangent, 0, 1),
+            segments.T,
+            segments,
+            gain_attn,
+            gain_mlp,
+            downs.T,
+            query_up_factor[0],
+            value_up_factor[0],
             jnp.swapaxes(joint_projection_weight[0], 0, 1),
-            ups,
             w_out[0],
             w_fc[0],
             w_proj[0],
         ),
     )
-    totals = []
-    for layer in (1, 0):
-        placed_up = [
-            lax.dynamic_update_slice_in_dim(
-                jnp.zeros((rank, model), F32),
-                up_sums[layer, k, k * rank : (k + 1) * rank],
-                (2 * y + core) * width,
-                1,
-            )
-            for k in range(2)
-        ]
-        total = jnp.concatenate([down_sums[layer, : 2 * rank], *placed_up], axis=0)
-        total = total + sent(total, lambda c, z, y, x: (1 - c, z, y, x))
-        total = total + sent(total, lambda c, z, y, x: (c, z, y, 1 - x))
-        total = total + sent(total, lambda c, z, y, x: (c, z, 1 - y, x))
-        bit = 1
-        while bit < planes:
-            total = total + sent(total, lambda c, z, y, x: (c, z ^ bit, y, x))
-            bit *= 2
-        totals.append(total)
-
-    def placed(pair):
-        same, other = [], []
-        for layer in range(2):
-            same.append(
-                sent(pair[layer], lambda c, z, y, x: (layer, z, y, x) if c == x else None)
-            )
-            other.append(
-                sent(pair[layer], lambda c, z, y, x: (layer, z, y, 1 - x) if c != x else None)
-            )
-        same = jnp.where(core_0, same[0], same[1])
-        other = jnp.where(core_0, other[0], other[1])
-        return jnp.stack([jnp.where(x_0, same, other), jnp.where(x_0, other, same)], axis=1)[None]
-
-    total = jnp.where(core_0, totals[1], totals[0])
     return (
-        placed(acts),
-        placed(grads),
+        jnp.swapaxes(acts, 0, 1)[None],
+        jnp.swapaxes(grads, 0, 1)[None],
         total[:rank].T[None],
         total[2 * rank : 3 * rank][None],
         total[rank : 2 * rank].T[None],
@@ -1196,6 +1353,7 @@
     return (
         mesh.shape["section"] == 2
         and mesh.shape["tensor"] == 4
+        and planes > 1
         and planes & (planes - 1) == 0
         and rows_all == 2 * planes
         and slots == 1024

time: 419 us -> 323 us (0.77)
  Pallas kernels: 332 us -> 303 us
  starting transfers between devices: 27.2 us -> 0 us
  waiting for transfers between devices: 22.9 us -> 0 us
  local copies, waits for them, and re-layouts: 19.6 us -> 11.3 us
  other arithmetic: 8.49 us -> 1.33 us
    pallas_call x1, Pallas kernels: 332 us -> 303 us  [step_call(): pl.pallas_call(functools.partial(step_kernel, block, model, planes), out_...]
    ppermute x18 -> x0, starting transfers between devices: 27.2 us -> none  [sent(): return lax.ppermute(value, ROUTE_AXES, route(planes, rule))]
    ppermute x18 -> x0, waiting for transfers between devices: 22.9 us -> none  [sent(): return lax.ppermute(value, ROUTE_AXES, route(planes, rule))]
    slice x2 -> x0, local copies, waits for them, and re-layouts: 4.9 us -> none  [both_rows(): array[:, 0]]
    select_n x5 -> x0, other arithmetic: 4.74 us -> none  [the longest x2 2.57 us: both_rows(): jnp.where(x_0, array[:, 1], array[:, 0])]
  transfers between devices with their start and end apart: 18 -> 0, of which waited for: 6 -> 0; matrix products, arithmetic and copies ran while one was open for 1% -> 0% of each run, Pallas kernels for 0% -> 0%
where the time goes in v3:
time: 323 us; the launch traced here: 317 us
  Pallas kernels  303 us (94%)
  local copies, waits for them, and re-layouts  11.3 us (3%)
    pallas_call x1, Pallas kernels, step_call(): pl.pallas_call(functools.partial(step_kernel, block, model, planes), out_...  303 us
    unnamed x7, local copies, waits for them, and re-layouts  7.13 us

profile of v3, /device:TPU:0, one launch (start us, length us, event | category | flops | bytes accessed | tf_op | source)
XLA Modules:
  0.0 316.6 jit_solution(2953804201429357765)
XLA Ops:
  0.6 1.3 maximum_bitcast_fusion.downs_t
  2.0 1.7 copy.21
  3.7 3.5 %copy_bitcast_fusion = (bf16[2,256,1024]{2,1,0:T(8,128)(2,1)}, bf16[2,256,1024]{2,1,0:T(8,128)(2,1)}) fusion(bf16[256,2,1024]{2,1,0:T(2,128)(2,1)} %param.15, bf16[256,2,1024]{2,1,0:T(2,128)(2,1)} %param.13), kind=kLoop, calls=%fused_computation | loop fusion | bytes 4194304 | tf_op jit(solution)/shard_map/transpose | solution.py:1326
  7.2 302.9 %shard_map.172 = (bf16[2,256,1024]{2,1,0:T(8,128)(2,1)}, bf16[2,256,1024]{2,1,0:T(8,128)(2,1)}, f32[16,1024]{1,0:T(8,128)}) custom-call(bf16[2,256,1024]{2,1,0:T(8,128)(2,1)} %get-tuple-element.23.x_rows, bf16[2,256,1024]{2,1,0:T(8,128)(2,1)} %get-tuple-element.22.cot_rows, s32[1024,2]{1,0:T(8,128)} %bitcast.35, s32[2,1024]{1,0:T(2,128)} %seg_rows.1, ...), custom_call_target="tpu_custom_call" | custom-call | tf_op jit(solution)/shard_map/pallas_call | solution.py:1234
  310.1 0.0 copy-start
  310.1 0.0 copy-start.1
  310.1 3.4 %copy.22 = bf16[1,256,2,1024]{3,2,1,0:T(2,128)(2,1)} copy(bf16[1,256,2,1024]{3,1,2,0:T(8,128)(2,1)} %bitcast.40) | data formatting | bytes 2097152
  313.5 0.0 copy-done
  313.5 2.0 copy.23
  315.5 0.0 copy-done.1
  315.5 0.6 slice_bitcast_fusion
Async XLA Ops:
  310.1 3.4 %copy-start = (bf16[2,256,1024]{2,1,0:T(8,128)(2,1)S(1)}, bf16[2,256,1024]{2,1,0:T(8,128)(2,1)}, u32[]{:S(2)}) copy-start(bf16[2,256,1024]{2,1,0:T(8,128)(2,1)} %get-tuple-element.10) | copy-start | bytes 3145732
  310.1 5.4 %copy-start.1 = (f32[16,1024]{1,0:T(8,128)S(1)}, f32[16,1024]{1,0:T(8,128)}, u32[]{:S(2)}) copy-start(f32[16,1024]{1,0:T(8,128)} %get-tuple-element.11) | copy-start | bytes 196612
